TPU v7x, 1024 devices: a whole 8x8x8 slice. The times are simulated.
1024 devices in a mesh: seq: 64 (over x_hi, z, core), chan: 16 (over y, x_lo).
Axes of the slice: x: 8 (x_hi: 4, x_lo: 2; x = x_hi * 2 + x_lo), y: 8, z: 8, core: 2. Of those that a mesh axis runs over, the one named last changes fastest.
Arguments:
- tokens: bfloat16 [20480, 4096], P('seq', 'chan'), may hold values from -70 to 70
- in_weight: bfloat16 [4096, 3, 4096], P(None, None, 'chan'), may hold values from -0.09375 to 0.09375
- short_filter: float32 [3, 3, 4096], P(None, None, 'chan'), may hold values from -2 to 2
- long_filter: bfloat16 [256, 128], P('chan'), may hold values from -0.5 to 0.5
- skip_gain: float32 [4096], P('chan'), may hold values from -4 to 4
- out_weight: bfloat16 [4096, 4096], P('chan'), may hold values from -0.125 to 0.125
Outputs:
- mixed: bfloat16 [20480, 4096], P('seq', 'chan')
All inputs are finite; a program needn't handle non-finite values.
Results may differ from a plain program's by a relative error of at most 0.018.
Values may be sent and summed in bfloat16 or wider, within the bound.
No kernel may reach another device: no remote copies, remote signals or barrier semaphores. Data moves between devices by JAX's collectives and lax.ppermute only.
A program may use at most 64 MiB of HBM per device.

v0:
```python
import jax
import jax.numpy as jnp
from jax import lax
from jax.experimental import pallas as pl
from jax.experimental.pallas import tpu as pltpu
from jax.sharding import PartitionSpec as P


YS = 8
XS = 2
LATE_IN = 128
LATE_OUT = 160
BLOCK = 32
HALO = 136
WIDE_FROM = 320 - LATE_OUT - 128 - 16
VMEM = pltpu.VMEM
F32 = jnp.float32
BF16 = jnp.bfloat16

Y_GROUPS = [[y * XS + x for y in range(YS)] for x in range(XS)]
X_PAIRS = [(y * XS + x, y * XS + 1 - x) for y in range(YS) for x in range(XS)]


def swap_x(value):
    return lax.ppermute(value, "chan", X_PAIRS)


def exchange_y(value):
    return lax.all_to_all(value, "chan", 0, 0, tiled=True, axis_index_groups=Y_GROUPS)


def shifted(value, axis):
    count = lax.axis_size(axis)
    return lax.ppermute(value, axis, [(source, source + 1) for source in range(count - 1)])


def in_vmem(value):
    return pltpu.with_memory_space_constraint(value, VMEM)


def squares_of(pieces):
    total = None
    for piece in pieces:
        wide = piece.astype(F32)
        wide = wide * wide
        part = wide[:, :128] + wide[:, 128:]
        total = part if total is None else total + part
    return total


def products(pieces, weights):
    total = None
    for piece, weight in zip(pieces, weights):
        part = jnp.dot(piece, weight, preferred_element_type=F32)
        total = part if total is None else total + part
    return total


def scale_of(squares):
    mean = jnp.sum(squares, axis=1, keepdims=True) / (YS * XS * 256)
    return lax.rsqrt(mean + 1e-06)


def start_all(copies):
    for copy in copies:
        copy.start()


def wait_all(copies):
    for copy in copies:
        copy.wait()


def own_kernel(
    x_ref, own_hbm, weight_hbm, taps, sum_hbm, squares_hbm, table_hbm,
    own, weight, sums, squares, table, arrived, sent
):
    x = x_ref[0]
    own_fetch = pltpu.make_async_copy(own_hbm, own, arrived.at[3])
    fetches = [
        pltpu.make_async_copy(weight_hbm.at[i, :, x], weight.at[i], arrived.at[i]) for i in range(3)
    ]
    start_all([own_fetch] + fetches)
    for g in range(16):
        line = jnp.broadcast_to(taps[g : g + 1, :], (BLOCK, 256))
        rolled = pltpu.roll(line, 1, 1, stride=1, stride_axis=0)
        table[BLOCK * g : BLOCK * g + BLOCK] = rolled.astype(BF16)
    own_fetch.wait()
    squares[...] = squares_of([own[y] for y in range(YS)])
    for i in range(3):
        fetches[i].wait()
        sums[i] = products([own[y] for y in range(YS)], [weight[i, y] for y in range(YS)])
    sends = [
        pltpu.make_async_copy(sums, sum_hbm, sent.at[0]),
        pltpu.make_async_copy(squares, squares_hbm, sent.at[1]),
        pltpu.make_async_copy(table, table_hbm, sent.at[2]),
    ]
    start_all(sends)
    wait_all(sends)


def other_kernel(
    x_ref, oth_hbm, weight_hbm, sum_hbm, squares_hbm, out_hbm,
    oth, weight, sums, squares, out, arrived, sent
):
    other = 1 - x_ref[0]
    oth_fetch = pltpu.make_async_copy(oth_hbm, oth, arrived.at[3])
    squares_fetch = pltpu.make_async_copy(squares_hbm, squares, arrived.at[4])
    sum_fetch = pltpu.make_async_copy(sum_hbm, sums, arrived.at[5])
    fetches = [
        pltpu.make_async_copy(weight_hbm.at[i, :, other], weight.at[i], arrived.at[i])
        for i in range(3)
    ]
    start_all([oth_fetch, squares_fetch, fetches[0], sum_fetch] + fetches[1:])
    oth_fetch.wait()
    squares_fetch.wait()
    scale = scale_of(squares[...] + squares_of([oth[y] for y in range(YS)]))
    for i in range(3):
        fetches[i].wait()
        part = products([oth[y] for y in range(YS)], [weight[i, y] for y in range(YS)])
        if i == 0:
            sum_fetch.wait()
        out[:, 256 * i : 256 * i + 256] = ((sums[i] + part) * scale).astype(BF16)
    send = pltpu.make_async_copy(out, out_hbm, sent)
    send.start()
    send.wait()


def late_kernel(x_ref, pair2, weight_hbm, proj_hbm, out_hbm, head, weight, out, arrived, sent):
    x = x_ref[0]
    late = pair2.shape[2]
    early = proj_hbm.shape[0]
    head_fetch = pltpu.make_async_copy(proj_hbm.at[early + late - HALO : early], head, arrived.at[3])
    fetches = [pltpu.make_async_copy(weight_hbm.at[i], weight.at[i], arrived.at[i]) for i in range(3)]
    start_all(fetches + [head_fetch])
    pieces = [pair2[y, side] for y in range(YS) for side in range(2)]
    scale = scale_of(squares_of(pieces))
    for i in range(3):
        fetches[i].wait()
        weights = [weight[i, y, side] for y in range(YS) for side in (x, 1 - x)]
        out[HALO - late :, 256 * i : 256 * i + 256] = (products(pieces, weights) * scale).astype(BF16)
    head_fetch.wait()
    out[0 : HALO - late] = head[...]
    send = pltpu.make_async_copy(out, out_hbm, sent)
    send.start()
    send.wait()


def mix_rows(wide, base, gated, table, short, skip, mixed, count):
    def stream(i, start, length):
        lanes = slice(256 * i, 256 * i + 256)
        total = short[0, i : i + 1, :] * wide[start : start + length, lanes]
        for back in range(1, 3):
            total += short[back, i : i + 1, :] * wide[start - back : start - back + length, lanes]
        return total

    product = stream(1, base, count + 128) * stream(2, base, count + 128)
    gated[0 : count + 128] = product.astype(BF16)
    gated[count + 128 :] = jnp.zeros((gated.shape[0] - count - 128, 256), BF16)
    group = lax.broadcasted_iota(jnp.int32, (BLOCK, 256), 1) // 16
    for b in range(count // BLOCK):
        window = gated[BLOCK * b : BLOCK * b + 256]
        every = jnp.dot(table[...], window, preferred_element_type=F32)
        total = every[0:BLOCK]
        for g in range(1, 16):
            total = jnp.where(group == g, every[BLOCK * g : BLOCK * g + BLOCK], total)
        own = gated[BLOCK * b + 128 : BLOCK * b + 128 + BLOCK].astype(F32)
        total = total + skip[...] * own
        queries = stream(0, base + 128 + BLOCK * b, BLOCK)
        mixed[BLOCK * b : BLOCK * b + BLOCK] = (queries * total).astype(BF16)


def out_rows(x, value, weight, store):
    for y in range(YS):
        mine = pl.multiple_of(y * 512 + x * 256, 256)
        other = pl.multiple_of(y * 512 + 256 - x * 256, 256)
        store(y, 0, jnp.dot(value, weight[:, pl.ds(mine, 256)], preferred_element_type=F32).astype(BF16))
        store(y, 1, jnp.dot(value, weight[:, pl.ds(other, 256)], preferred_element_type=F32).astype(BF16))


def inner_kernel(
    x_ref, proj_hbm, tail_hbm, table_hbm, short, skip, out_hbm, pair_hbm,
    proj1, tail, table, out_weight, wide, gated, mixed, pair, arrived, sent
):
    proj_fetch = pltpu.make_async_copy(proj_hbm.at[WIDE_FROM:], proj1, arrived.at[0])
    tail_fetch = pltpu.make_async_copy(tail_hbm.at[HALO - LATE_IN :], tail, arrived.at[1])
    table_fetch = pltpu.make_async_copy(table_hbm, table, arrived.at[2])
    out_fetch = pltpu.make_async_copy(out_hbm, out_weight, arrived.at[3])
    start_all([proj_fetch, tail_fetch, table_fetch, out_fetch])
    count = proj1.shape[0]
    proj_fetch.wait()
    wide[0:count] = proj1[...].astype(F32)
    tail_fetch.wait()
    wide[count:] = tail[...].astype(F32)
    table_fetch.wait()
    mix_rows(wide, 16, gated, table, short, skip, mixed, LATE_OUT)
    out_fetch.wait()
    sends = [pltpu.make_async_copy(pair.at[y], pair_hbm.at[y], sent.at[y]) for y in range(YS)]

    def place(y, side, value):
        pair[y, side] = value
        if side == 1:
            sends[y].start()

    out_rows(x_ref[0], mixed[...], out_weight, place)
    wait_all(sends)


def edge_kernel(
    x_ref, halo, proj_hbm, table_hbm, short, skip, out_hbm, send_hbm, keep_hbm,
    proj1, table, out_weight, wide, gated, mixed, send, keep, arrived, sent
):
    count = mixed.shape[0]
    proj_fetch = pltpu.make_async_copy(proj_hbm.at[0:count], proj1, arrived.at[0])
    table_fetch = pltpu.make_async_copy(table_hbm, table, arrived.at[1])
    out_fetch = pltpu.make_async_copy(out_hbm, out_weight, arrived.at[2])
    for fetch in (proj_fetch, table_fetch, out_fetch):
        fetch.start()
    wide[0:HALO] = halo[...].astype(F32)
    proj_fetch.wait()
    wide[HALO:] = proj1[...].astype(F32)
    table_fetch.wait()
    mix_rows(wide, HALO - 128, gated, table, short, skip, mixed, count)
    out_fetch.wait()

    sends = [pltpu.make_async_copy(send.at[y], send_hbm.at[y], sent.at[y]) for y in range(YS)]
    keeps = [pltpu.make_async_copy(keep.at[y], keep_hbm.at[y], sent.at[YS + y]) for y in range(YS)]

    def place(y, side, value):
        if side == 0:
            keep[y] = value
            keeps[y].start()
        else:
            send[y] = value
            sends[y].start()

    out_rows(x_ref[0], mixed[...], out_weight, place)
    wait_all(sends + keeps)


WHOLE = pl.BlockSpec(memory_space=VMEM)
ANY = pl.BlockSpec(memory_space=pltpu.HBM)
SCALAR = pl.BlockSpec(memory_space=pltpu.SMEM)
PARAMS = pltpu.CompilerParams(vmem_limit_bytes=55 << 20)


def struct(*shape):
    return jax.ShapeDtypeStruct(shape, BF16)


def body(tokens, in_weight, short_filter, long_filter, skip_gain, out_weight):
    rows = tokens.shape[0]
    early_in = rows - LATE_IN
    early_out = rows - LATE_OUT
    x = (lax.axis_index("chan") % XS).astype(jnp.int32)[None]
    weight = jnp.transpose(in_weight, (1, 0, 2)).reshape(3, YS, XS, 256, 256)
    taps = jnp.pad(jnp.flip(long_filter, 1).astype(F32), ((0, 0), (0, 128)))
    skip = skip_gain[None]

    top, tail = tokens[:early_in], tokens[early_in:]
    tail_other = swap_x(tail)
    own1 = exchange_y(jnp.broadcast_to(top[None], (YS,) + top.shape))
    oth1 = swap_x(own1)
    both = jnp.stack([tail, tail_other])
    both = jnp.broadcast_to(both[None], (YS,) + both.shape)
    pair2 = exchange_y(both)

    half_space = VMEM((3, YS, 256, 256), BF16)
    table_space = VMEM((16 * BLOCK, 256), BF16)
    out_space = VMEM(out_weight.shape, BF16)
    sum_shape = (3, early_in, 256)
    copies = pltpu.SemaphoreType.DMA
    sums, squares, table = pl.pallas_call(
        own_kernel,
        in_specs=[SCALAR, ANY, ANY, WHOLE],
        out_specs=[ANY] * 3,
        out_shape=[
            jax.ShapeDtypeStruct(sum_shape, F32),
            jax.ShapeDtypeStruct((early_in, 128), F32),
            struct(16 * BLOCK, 256),
        ],
        scratch_shapes=[
            VMEM(own1.shape, BF16),
            half_space,
            VMEM(sum_shape, F32),
            VMEM((early_in, 128), F32),
            table_space,
            copies((4,)),
            copies((3,)),
        ],
        compiler_params=PARAMS,
        name="own",
    )(x, own1, weight, taps)
    proj1 = pl.pallas_call(
        other_kernel,
        in_specs=[SCALAR, ANY, ANY, ANY, ANY],
        out_specs=ANY,
        out_shape=struct(early_in, 768),
        scratch_shapes=[
            VMEM(oth1.shape, BF16),
            half_space,
            VMEM(sum_shape, F32),
            VMEM((early_in, 128), F32),
            VMEM((early_in, 768), BF16),
            copies((6,)),
            copies,
        ],
        compiler_params=PARAMS,
        name="other",
    )(x, oth1, weight, sums, squares)
    tail_rows = pl.pallas_call(
        late_kernel,
        in_specs=[SCALAR, WHOLE, ANY, ANY],
        out_specs=ANY,
        out_shape=struct(HALO, 768),
        scratch_shapes=[
            VMEM((HALO - LATE_IN, 768), BF16),
            VMEM(weight.shape, BF16),
            VMEM((HALO, 768), BF16),
            copies((4,)),
            copies,
        ],
        compiler_params=PARAMS,
        name="late",
    )(x, in_vmem(pair2), weight, proj1)
    pair = pl.pallas_call(
        inner_kernel,
        in_specs=[SCALAR, ANY, ANY, ANY, WHOLE, WHOLE, ANY],
        out_specs=ANY,
        out_shape=struct(YS, 2, LATE_OUT, 256),
        scratch_shapes=[
            VMEM((early_in - WIDE_FROM, 768), BF16),
            VMEM((LATE_IN, 768), BF16),
            table_space,
            out_space,
            VMEM((rows - WIDE_FROM, 768), F32),
            VMEM((LATE_OUT + 256, 256), BF16),
            VMEM((LATE_OUT, 256), BF16),
            VMEM((YS, 2, LATE_OUT, 256), BF16),
            copies((4,)),
            copies((YS,)),
        ],
        compiler_params=PARAMS,
        name="inner",
    )(x, proj1, tail_rows, table, short_filter, skip, out_weight)

    halo = shifted(tail_rows, "seq")
    pair = exchange_y(pair)
    send, keep = pl.pallas_call(
        edge_kernel,
        in_specs=[SCALAR, WHOLE, ANY, ANY, WHOLE, WHOLE, ANY],
        out_specs=[ANY] * 2,
        out_shape=[struct(YS, early_out, 256), struct(YS, early_out, 256)],
        scratch_shapes=[
            VMEM((early_out, 768), BF16),
            table_space,
            out_space,
            VMEM((HALO + early_out, 768), F32),
            VMEM((early_out + 256, 256), BF16),
            VMEM((early_out, 256), BF16),
            VMEM((YS, early_out, 256), BF16),
            VMEM((YS, early_out, 256), BF16),
            copies((3,)),
            copies((2 * YS,)),
        ],
        compiler_params=PARAMS,
        name="edge",
    )(x, in_vmem(halo), proj1, table, short_filter, skip, out_weight)

    received = swap_x(send)
    sums = jnp.sum(pair.astype(F32), axis=0)
    late_send = sums[1].astype(BF16)
    late_received = swap_x(late_send)
    merged = (keep.astype(F32) + received.astype(F32)).astype(BF16)
    merged = exchange_y(merged)
    early_sum = jnp.sum(merged.astype(F32), axis=0).astype(BF16)
    late_sum = (sums[0] + late_received.astype(F32)).astype(BF16)
    return jnp.concatenate([early_sum, late_sum], axis=0)


def solution(mesh):
    in_specs = (
        P("seq", "chan"),
        P(None, None, "chan"),
        P(None, None, "chan"),
        P("chan", None),
        P("chan"),
        P("chan", None),
    )
    out_specs = P("seq", "chan")
    return jax.shard_map(body, mesh=mesh, in_specs=in_specs, out_specs=out_specs, check_vma=False)
```

profile of v0, /device:TPU:14, one launch (start us, length us, event | category | flops | bytes accessed | tf_op | source)
XLA Modules:
  0.0 144.5 jit_solution(5103432171509179390)
XLA Ops:
  0.0 0.9 slice.14
  0.9 1.0 broadcast_in_dim.20
  1.9 7.6 %all-to-all-start.1 = ((bf16[8,192,256]{2,1,0:T(8,128)(2,1)}), bf16[8,192,256]{2,1,0:T(8,128)(2,1)S(1)}, u32[]{:S(2)}, u32[]{:S(2)}) async-start(bf16[8,192,256]{2,1,0:T(8,128)(2,1)} %broadcast_in_dim.20), calls=%async_computation.1 | async-start | bytes 1572864 | tf_op jit(solution)/shard_map/all_to_all | solution.py:29
  9.4 0.8 slice_bitcast_fusion.1
  10.3 3.3 %collective-permute-start = (bf16[128,256]{1,0:T(8,128)(2,1)S(1)}, bf16[128,256]{1,0:T(8,128)(2,1)S(1)}, u32[]{:S(2)}, u32[]{:S(2)}) collective-permute-start(bf16[128,256]{1,0:T(8,128)(2,1)S(1)} %get-tuple-element.16), channel_id=1, source_target_pairs={{0,1},{1,0},{2,3},{3,2},{4,5},{5,4},{6,7},{7,6},{8,9},{9,8},{10,11... | collective-permute-start | bytes 196616 | tf_op jit(solution)/shard_map/ppermute | solution.py:25
  13.6 2.8 %collective-permute-done = bf16[128,256]{1,0:T(8,128)(2,1)S(1)} collective-permute-done((bf16[128,256]{1,0:T(8,128)(2,1)S(1)}, bf16[128,256]{1,0:T(8,128)(2,1)S(1)}, u32[]{:S(2)}, u32[]{:S(2)}) %collective-permute-start) | collective-permute-done | bytes 65568 | tf_op jit(solution)/shard_map/ppermute | solution.py:25
  16.4 16.1 %all-to-all-done.1.own_hbm = bf16[8,192,256]{2,1,0:T(8,128)(2,1)S(1)} async-done(((bf16[8,192,256]{2,1,0:T(8,128)(2,1)}), bf16[8,192,256]{2,1,0:T(8,128)(2,1)S(1)}, u32[]{:S(2)}, u32[]{:S(2)}) %all-to-all-start.1) | async-done | bytes 786464 | tf_op jit(solution)/shard_map/all_to_all | solution.py:29
  32.5 1.2 broadcast_in_dim.9
  33.7 3.7 %all-to-all-start = ((bf16[8,2,128,256]{3,2,1,0:T(8,128)(2,1)}), bf16[8,2,128,256]{3,2,1,0:T(8,128)(2,1)S(1)}, u32[]{:S(2)}, u32[]{:S(2)}) async-start(bf16[8,2,128,256]{3,2,1,0:T(8,128)(2,1)} %broadcast_in_dim.9), calls=%async_computation | async-start | bytes 2097152 | tf_op jit(solution)/shard_map/all_to_all | solution.py:29
  37.4 3.3 %collective-permute-start.1 = (bf16[8,192,256]{2,1,0:T(8,128)(2,1)S(1)}, bf16[8,192,256]{2,1,0:T(8,128)(2,1)S(1)}, u32[]{:S(2)}, u32[]{:S(2)}) collective-permute-start(bf16[8,192,256]{2,1,0:T(8,128)(2,1)S(1)} %all-to-all-done.1.own_hbm), channel_id=1, source_target_pairs={{0,1},{1,0},{2,3},{3,2},{4,5},{5,4},{6,7},{7,6},{8,9},{9,8},{10,11... | collective-permute-start | bytes 2359304 | tf_op jit(solution)/shard_map/ppermute | solution.py:25
  40.8 0.1 rev.4
  40.9 0.6 pad_convert_fusion.taps
  41.5 4.7 %own.1 = (f32[3,192,256]{2,1,0:T(8,128)}, f32[192,128]{1,0:T(8,128)}, bf16[512,256]{1,0:T(8,128)(2,1)}) custom-call(s32[1]{0:T(128)} %bitcast.x_ref, bf16[8,192,256]{2,1,0:T(8,128)(2,1)} %copy-done, bf16[3,8,2,256,256]{4,3,2,1,0:T(8,128)(2,1)} %bitcast.16, f32[16,256]{1,0:T(8,128)} %pad_convert_fusion.taps), custom_call_target="tpu_custom_call" | custom-call | tf_op jit(solution)/shard_map/own/pallas_call | solution.py:273
  46.2 12.6 %collective-permute-done.1.oth_hbm = bf16[8,192,256]{2,1,0:T(8,128)(2,1)S(1)} collective-permute-done((bf16[8,192,256]{2,1,0:T(8,128)(2,1)S(1)}, bf16[8,192,256]{2,1,0:T(8,128)(2,1)S(1)}, u32[]{:S(2)}, u32[]{:S(2)}) %collective-permute-start.1) | collective-permute-done | bytes 786464 | tf_op jit(solution)/shard_map/ppermute | solution.py:25
  58.8 0.9 copy-done.2
  59.7 3.9 %other.1.proj_hbm = bf16[192,768]{1,0:T(8,128)(2,1)} custom-call(s32[1]{0:T(128)} %bitcast.x_ref, bf16[8,192,256]{2,1,0:T(8,128)(2,1)} %copy-done.2, bf16[3,8,2,256,256]{4,3,2,1,0:T(8,128)(2,1)} %bitcast.17, f32[3,192,256]{2,1,0:T(8,128)} %get-tuple-element.10.sum_hbm, f32[192,128]{1,0:T(8,128)} %get-tuple-element.11.squares_hbm), custom_call_target="tpu_custom_call" | custom-call | tf_op jit(solution)/shard_map/other/pallas_call | solution.py:294
  63.6 2.9 %all-to-all-done.pair2 = bf16[8,2,128,256]{3,2,1,0:T(8,128)(2,1)S(1)} async-done(((bf16[8,2,128,256]{3,2,1,0:T(8,128)(2,1)}), bf16[8,2,128,256]{3,2,1,0:T(8,128)(2,1)S(1)}, u32[]{:S(2)}, u32[]{:S(2)}) %all-to-all-start) | async-done | bytes 1048608 | tf_op jit(solution)/shard_map/all_to_all | solution.py:29
  66.6 4.5 %late.1.tail_hbm = bf16[136,768]{1,0:T(8,128)(2,1)} custom-call(s32[1]{0:T(128)} %bitcast.x_ref, bf16[8,2,128,256]{3,2,1,0:T(8,128)(2,1)S(1)} %all-to-all-done.pair2, bf16[3,8,2,256,256]{4,3,2,1,0:T(8,128)(2,1)} %bitcast.18, bf16[192,768]{1,0:T(8,128)(2,1)} %other.1.proj_hbm), custom_call_target="tpu_custom_call" | custom-call | tf_op jit(solution)/shard_map/late/pallas_call | solution.py:311
  71.1 4.0 %inner.1 = bf16[8,2,160,256]{3,2,1,0:T(8,128)(2,1)} custom-call(s32[1]{0:T(128)} %bitcast.x_ref, bf16[192,768]{1,0:T(8,128)(2,1)} %other.1.proj_hbm, bf16[136,768]{1,0:T(8,128)(2,1)} %late.1.tail_hbm, bf16[512,256]{1,0:T(8,128)(2,1)} %get-tuple-element.12.table_hbm, f32[3,3,256]{2,1,0:T(4,128)} %short.3, f32[1,256]{1,0:T(1,128)} %bitcast.20, ...), custom_call_target="tpu_custom_call" | custom-call | tf_op jit(solution)/shard_map/inner/pallas_call | solution.py:326
  75.2 4.0 %all-to-all-start.3 = ((bf16[8,2,160,256]{3,2,1,0:T(8,128)(2,1)}), bf16[8,2,160,256]{3,2,1,0:T(8,128)(2,1)S(1)}, u32[]{:S(2)}, u32[]{:S(2)}) async-start(bf16[8,2,160,256]{3,2,1,0:T(8,128)(2,1)} %inner.1), calls=%async_computation.3 | async-start | bytes 2621440 | tf_op jit(solution)/shard_map/all_to_all | solution.py:29
  79.2 1.9 %collective-permute-start.2 = (bf16[136,768]{1,0:T(8,128)(2,1)S(1)}, bf16[136,768]{1,0:T(8,128)(2,1)S(1)}, u32[]{:S(2)}, u32[]{:S(2)}) collective-permute-start(bf16[136,768]{1,0:T(8,128)(2,1)S(1)} %copy-done.1), channel_id=1, source_target_pairs={{0,16},{16,32},{32,48},{48,64},{64,80},{80,96},{96,112},{112,128},... | collective-permute-start | bytes 626696 | tf_op jit(solution)/shard_map/ppermute | solution.py:34
  81.1 22.2 %collective-permute-done.2.halo = bf16[136,768]{1,0:T(8,128)(2,1)S(1)} collective-permute-done((bf16[136,768]{1,0:T(8,128)(2,1)S(1)}, bf16[136,768]{1,0:T(8,128)(2,1)S(1)}, u32[]{:S(2)}, u32[]{:S(2)}) %collective-permute-start.2) | collective-permute-done | bytes 208928 | tf_op jit(solution)/shard_map/ppermute | solution.py:34
  103.4 4.0 %edge.1 = (bf16[8,160,256]{2,1,0:T(8,128)(2,1)}, bf16[8,160,256]{2,1,0:T(8,128)(2,1)}) custom-call(s32[1]{0:T(128)} %bitcast.x_ref, bf16[136,768]{1,0:T(8,128)(2,1)S(1)} %collective-permute-done.2.halo, bf16[192,768]{1,0:T(8,128)(2,1)} %other.1.proj_hbm, bf16[512,256]{1,0:T(8,128)(2,1)} %get-tuple-element.12.table_hbm, f32[3,3,256]{2,1,0:T(4,128)} %short.3, ...), custom_call_target="tpu_custom_call" | custom-call | tf_op jit(solution)/shard_map/edge/pallas_call | solution.py:349
  107.4 1.9 %collective-permute-start.3 = (bf16[8,160,256]{2,1,0:T(8,128)(2,1)}, bf16[8,160,256]{2,1,0:T(8,128)(2,1)S(1)}, u32[]{:S(2)}, u32[]{:S(2)}) collective-permute-start(bf16[8,160,256]{2,1,0:T(8,128)(2,1)} %get-tuple-element.14), channel_id=1, source_target_pairs={{0,1},{1,0},{2,3},{3,2},{4,5},{5,4},{6,7},{7,6},{8,9},{9,8},{10,11... | collective-permute-start | bytes 1966088 | tf_op jit(solution)/shard_map/ppermute | solution.py:25
  109.3 10.8 %collective-permute-done.3 = bf16[8,160,256]{2,1,0:T(8,128)(2,1)S(1)} collective-permute-done((bf16[8,160,256]{2,1,0:T(8,128)(2,1)}, bf16[8,160,256]{2,1,0:T(8,128)(2,1)S(1)}, u32[]{:S(2)}, u32[]{:S(2)}) %collective-permute-start.3) | collective-permute-done | bytes 655392 | tf_op jit(solution)/shard_map/ppermute | solution.py:25
  120.1 2.1 %add_convert_fusion = bf16[8,160,256]{2,1,0:T(8,128)(2,1)} fusion(bf16[8,160,256]{2,1,0:T(8,128)(2,1)S(1)} %collective-permute-done.3, bf16[8,160,256]{2,1,0:T(8,128)(2,1)} %get-tuple-element.13), kind=kLoop, calls=%fused_computation.1 | loop fusion | flops 1310720 | bytes 1966080 | tf_op jit(solution)/shard_map/convert_element_type | solution.py:374
  122.2 6.8 %all-to-all-start.2 = ((bf16[8,160,256]{2,1,0:T(8,128)(2,1)}), bf16[8,160,256]{2,1,0:T(8,128)(2,1)S(1)}, u32[]{:S(2)}, u32[]{:S(2)}) async-start(bf16[8,160,256]{2,1,0:T(8,128)(2,1)} %add_convert_fusion), calls=%async_computation.2 | async-start | bytes 1310720 | tf_op jit(solution)/shard_map/all_to_all | solution.py:29
  129.0 0.2 convert_reduce_fusion
  129.2 1.9 %collective-permute-start.4 = (bf16[160,256]{1,0:T(8,128)(2,1)S(1)}, bf16[160,256]{1,0:T(8,128)(2,1)S(1)}, u32[]{:S(2)}, u32[]{:S(2)}) collective-permute-start(bf16[160,256]{1,0:T(8,128)(2,1)S(1)} %fusion.2), channel_id=1, source_target_pairs={{0,1},{1,0},{2,3},{3,2},{4,5},{5,4},{6,7},{7,6},{8,9},{9,8},{10,11... | collective-permute-start | bytes 245768 | tf_op jit(solution)/shard_map/ppermute | solution.py:25
  131.1 12.6 %all-to-all-done.2 = bf16[8,160,256]{2,1,0:T(8,128)(2,1)S(1)} async-done(((bf16[8,160,256]{2,1,0:T(8,128)(2,1)}), bf16[8,160,256]{2,1,0:T(8,128)(2,1)S(1)}, u32[]{:S(2)}, u32[]{:S(2)}) %all-to-all-start.2) | async-done | bytes 655392 | tf_op jit(solution)/shard_map/all_to_all | solution.py:29
  143.7 0.1 reduce_sum.21
  143.8 0.7 pad_maximum_fusion
  (12 shorter events, 0.1 us)
Async XLA Ops:
  1.9 30.7 %all-to-all-start.1 = ((bf16[8,192,256]{2,1,0:T(8,128)(2,1)}), bf16[8,192,256]{2,1,0:T(8,128)(2,1)S(1)}, u32[]{:S(2)}, u32[]{:S(2)}) async-start(bf16[8,192,256]{2,1,0:T(8,128)(2,1)} %broadcast_in_dim.20), calls=%async_computation.1 | async-start | bytes 1572864 | tf_op jit(solution)/shard_map/all_to_all | solution.py:29
  10.3 6.2 %collective-permute-start = (bf16[128,256]{1,0:T(8,128)(2,1)S(1)}, bf16[128,256]{1,0:T(8,128)(2,1)S(1)}, u32[]{:S(2)}, u32[]{:S(2)}) collective-permute-start(bf16[128,256]{1,0:T(8,128)(2,1)S(1)} %get-tuple-element.16), channel_id=1, source_target_pairs={{0,1},{1,0},{2,3},{3,2},{4,5},{5,4},{6,7},{7,6},{8,9},{9,8},{10,11... | collective-permute-start | bytes 196616 | tf_op jit(solution)/shard_map/ppermute | solution.py:25
  32.5 4.9 %copy-start = (bf16[8,192,256]{2,1,0:T(8,128)(2,1)}, bf16[8,192,256]{2,1,0:T(8,128)(2,1)S(1)}, u32[]{:S(2)}) copy-start(bf16[8,192,256]{2,1,0:T(8,128)(2,1)S(1)} %all-to-all-done.1.own_hbm) | copy-start | bytes 2359300
  33.7 7.1 %copy-start.3 = (bf16[16,128]{1,0:T(8,128)(2,1)S(1)}, bf16[16,128]{1,0:T(8,128)(2,1)}, u32[]{:S(2)}) copy-start(bf16[16,128]{1,0:T(8,128)(2,1)} %param.9) | copy-start | bytes 12292
  33.7 32.8 %all-to-all-start = ((bf16[8,2,128,256]{3,2,1,0:T(8,128)(2,1)}), bf16[8,2,128,256]{3,2,1,0:T(8,128)(2,1)S(1)}, u32[]{:S(2)}, u32[]{:S(2)}) async-start(bf16[8,2,128,256]{3,2,1,0:T(8,128)(2,1)} %broadcast_in_dim.9), calls=%async_computation | async-start | bytes 2097152 | tf_op jit(solution)/shard_map/all_to_all | solution.py:29
  37.4 21.4 %collective-permute-start.1 = (bf16[8,192,256]{2,1,0:T(8,128)(2,1)S(1)}, bf16[8,192,256]{2,1,0:T(8,128)(2,1)S(1)}, u32[]{:S(2)}, u32[]{:S(2)}) collective-permute-start(bf16[8,192,256]{2,1,0:T(8,128)(2,1)S(1)} %all-to-all-done.1.own_hbm), channel_id=1, source_target_pairs={{0,1},{1,0},{2,3},{3,2},{4,5},{5,4},{6,7},{7,6},{8,9},{9,8},{10,11... | collective-permute-start | bytes 2359304 | tf_op jit(solution)/shard_map/ppermute | solution.py:25
  58.8 0.9 copy-start.2
  75.1 4.1 %copy-start.1 = (bf16[136,768]{1,0:T(8,128)(2,1)S(1)}, bf16[136,768]{1,0:T(8,128)(2,1)}, u32[]{:S(2)}) copy-start(bf16[136,768]{1,0:T(8,128)(2,1)} %late.1.tail_hbm) | copy-start | bytes 626692
  75.2 47.0 %all-to-all-start.3 = ((bf16[8,2,160,256]{3,2,1,0:T(8,128)(2,1)}), bf16[8,2,160,256]{3,2,1,0:T(8,128)(2,1)S(1)}, u32[]{:S(2)}, u32[]{:S(2)}) async-start(bf16[8,2,160,256]{3,2,1,0:T(8,128)(2,1)} %inner.1), calls=%async_computation.3 | async-start | bytes 2621440 | tf_op jit(solution)/shard_map/all_to_all | solution.py:29
  79.2 24.2 %collective-permute-start.2 = (bf16[136,768]{1,0:T(8,128)(2,1)S(1)}, bf16[136,768]{1,0:T(8,128)(2,1)S(1)}, u32[]{:S(2)}, u32[]{:S(2)}) collective-permute-start(bf16[136,768]{1,0:T(8,128)(2,1)S(1)} %copy-done.1), channel_id=1, source_target_pairs={{0,16},{16,32},{32,48},{48,64},{64,80},{80,96},{96,112},{112,128},... | collective-permute-start | bytes 626696 | tf_op jit(solution)/shard_map/ppermute | solution.py:34
  107.4 12.7 %collective-permute-start.3 = (bf16[8,160,256]{2,1,0:T(8,128)(2,1)}, bf16[8,160,256]{2,1,0:T(8,128)(2,1)S(1)}, u32[]{:S(2)}, u32[]{:S(2)}) collective-permute-start(bf16[8,160,256]{2,1,0:T(8,128)(2,1)} %get-tuple-element.14), channel_id=1, source_target_pairs={{0,1},{1,0},{2,3},{3,2},{4,5},{5,4},{6,7},{7,6},{8,9},{9,8},{10,11... | collective-permute-start | bytes 1966088 | tf_op jit(solution)/shard_map/ppermute | solution.py:25
  122.2 21.5 %all-to-all-start.2 = ((bf16[8,160,256]{2,1,0:T(8,128)(2,1)}), bf16[8,160,256]{2,1,0:T(8,128)(2,1)S(1)}, u32[]{:S(2)}, u32[]{:S(2)}) async-start(bf16[8,160,256]{2,1,0:T(8,128)(2,1)} %add_convert_fusion), calls=%async_computation.2 | async-start | bytes 1310720 | tf_op jit(solution)/shard_map/all_to_all | solution.py:29
  129.2 14.6 %collective-permute-start.4 = (bf16[160,256]{1,0:T(8,128)(2,1)S(1)}, bf16[160,256]{1,0:T(8,128)(2,1)S(1)}, u32[]{:S(2)}, u32[]{:S(2)}) collective-permute-start(bf16[160,256]{1,0:T(8,128)(2,1)S(1)} %fusion.2), channel_id=1, source_target_pairs={{0,1},{1,0},{2,3},{3,2},{4,5},{5,4},{6,7},{7,6},{8,9},{9,8},{10,11... | collective-permute-start | bytes 245768 | tf_op jit(solution)/shard_map/ppermute | solution.py:25
where the time goes:
time: 145 us
  waiting for transfers between devices  80 us (55%)
  starting transfers between devices  34.6 us (24%)
  Pallas kernels  21.2 us (15%)
  local copies, waits for them, and re-layouts  4.94 us (3%)
  other arithmetic  3.67 us (3%)
    all_to_all x4, waiting for transfers between devices, exchange_y(): lax.all_to_all(value, 'chan', 0, 0, tiled=True, axis_index_groups=Y_GROUPS)  31.6 us
    ppermute x4, waiting for transfers between devices, swap_x(): return lax.ppermute(value, 'chan', X_PAIRS)  26.2 us
    ppermute x1, waiting for transfers between devices, shifted(): lax.ppermute(value, axis, [(source, source + 1) for source in range(count...  22.2 us
    all_to_all x4, starting transfers between devices, exchange_y(): lax.all_to_all(value, 'chan', 0, 0, tiled=True, axis_index_groups=Y_GROUPS)  22.1 us
    ppermute x4, starting transfers between devices, swap_x(): return lax.ppermute(value, 'chan', X_PAIRS)  10.5 us
    pallas_call x1, Pallas kernels, body(): pl.pallas_call(own_kernel, in_specs=[SCALAR, ANY, ANY, WHOLE], out_specs=...  4.68 us
    pallas_call x1, Pallas kernels, body(): pl.pallas_call(late_kernel, in_specs=[SCALAR, WHOLE, ANY, ANY], out_specs...  4.52 us
    pallas_call x1, Pallas kernels, body(): pl.pallas_call(inner_kernel, in_specs=[SCALAR, ANY, ANY, ANY, WHOLE, WHOL...  4.05 us
  transfers between devices with their start and end apart: 9, of which 7 were waited for; matrix products, arithmetic and copies ran while one was open for 3% of the time, Pallas kernels for 9%

commit v1 on v0

--- a/solution.py
+++ b/solution.py
@@ -8,9 +8,9 @@
 
 YS = 8
 XS = 2
-LATE_IN = 128
-LATE_OUT = 160
-BLOCK = 32
+LATE_IN = 112
+LATE_OUT = 144
+BLOCK = 16
 HALO = 136
 WIDE_FROM = 320 - LATE_OUT - 128 - 16
 VMEM = pltpu.VMEM
@@ -69,6 +69,15 @@
 def wait_all(copies):
     for copy in copies:
         copy.wait()
+
+
+def spread_kernel(rows_hbm, out_hbm, sent):
+    copies = [
+        pltpu.make_async_copy(rows_hbm.at[0 : out_hbm.shape[1]], out_hbm.at[y], sent.at[y])
+        for y in range(YS)
+    ]
+    start_all(copies)
+    wait_all(copies)
 
 
 def own_kernel(
@@ -100,19 +109,17 @@
 
 
 def other_kernel(
-    x_ref, oth_hbm, weight_hbm, sum_hbm, squares_hbm, out_hbm,
-    oth, weight, sums, squares, out, arrived, sent
+    x_ref, oth, weight_hbm, sum_hbm, squares_hbm, out_hbm,
+    weight, sums, squares, out, arrived, sent
 ):
     other = 1 - x_ref[0]
-    oth_fetch = pltpu.make_async_copy(oth_hbm, oth, arrived.at[3])
-    squares_fetch = pltpu.make_async_copy(squares_hbm, squares, arrived.at[4])
-    sum_fetch = pltpu.make_async_copy(sum_hbm, sums, arrived.at[5])
+    squares_fetch = pltpu.make_async_copy(squares_hbm, squares, arrived.at[3])
+    sum_fetch = pltpu.make_async_copy(sum_hbm, sums, arrived.at[4])
     fetches = [
         pltpu.make_async_copy(weight_hbm.at[i, :, other], weight.at[i], arrived.at[i])
         for i in range(3)
     ]
-    start_all([oth_fetch, squares_fetch, fetches[0], sum_fetch] + fetches[1:])
-    oth_fetch.wait()
+    start_all([squares_fetch, fetches[0], sum_fetch] + fetches[1:])
     squares_fetch.wait()
     scale = scale_of(squares[...] + squares_of([oth[y] for y in range(YS)]))
     for i in range(3):
@@ -257,9 +264,19 @@
     taps = jnp.pad(jnp.flip(long_filter, 1).astype(F32), ((0, 0), (0, 128)))
     skip = skip_gain[None]
 
-    top, tail = tokens[:early_in], tokens[early_in:]
+    copies = pltpu.SemaphoreType.DMA
+    tail = tokens[early_in:]
+    top = pl.pallas_call(
+        spread_kernel,
+        in_specs=[ANY],
+        out_specs=ANY,
+        out_shape=struct(YS, early_in, 256),
+        scratch_shapes=[copies((YS,))],
+        compiler_params=PARAMS,
+        name="top",
+    )(tokens)
     tail_other = swap_x(tail)
-    own1 = exchange_y(jnp.broadcast_to(top[None], (YS,) + top.shape))
+    own1 = exchange_y(top)
     oth1 = swap_x(own1)
     both = jnp.stack([tail, tail_other])
     both = jnp.broadcast_to(both[None], (YS,) + both.shape)
@@ -269,7 +286,6 @@
     table_space = VMEM((16 * BLOCK, 256), BF16)
     out_space = VMEM(out_weight.shape, BF16)
     sum_shape = (3, early_in, 256)
-    copies = pltpu.SemaphoreType.DMA
     sums, squares, table = pl.pallas_call(
         own_kernel,
         in_specs=[SCALAR, ANY, ANY, WHOLE],
@@ -293,21 +309,20 @@
     )(x, own1, weight, taps)
     proj1 = pl.pallas_call(
         other_kernel,
-        in_specs=[SCALAR, ANY, ANY, ANY, ANY],
+        in_specs=[SCALAR, WHOLE, ANY, ANY, ANY],
         out_specs=ANY,
         out_shape=struct(early_in, 768),
         scratch_shapes=[
-            VMEM(oth1.shape, BF16),
             half_space,
             VMEM(sum_shape, F32),
             VMEM((early_in, 128), F32),
             VMEM((early_in, 768), BF16),
-            copies((6,)),
+            copies((5,)),
             copies,
         ],
         compiler_params=PARAMS,
         name="other",
-    )(x, oth1, weight, sums, squares)
+    )(x, in_vmem(oth1), weight, sums, squares)
     tail_rows = pl.pallas_call(
         late_kernel,
         in_specs=[SCALAR, WHOLE, ANY, ANY],

time: 145 us -> 173 us (1.19)
  Pallas kernels: 21.2 us -> 47.9 us
  local copies, waits for them, and re-layouts: 4.94 us -> 2 us
  starting transfers between devices: 34.6 us -> 37.4 us
    pallas_call x1 -> x2, Pallas kernels: 3.9 us -> 30.8 us  [the longest x1 27 us: body(): pl.pallas_call(spread_kernel, in_specs=[ANY], out_specs=ANY, out_shape=st...]
    ppermute x4, waiting for transfers between devices: 26.2 us -> 33.2 us  [swap_x(): return lax.ppermute(value, 'chan', X_PAIRS)]
    all_to_all x4, waiting for transfers between devices: 31.6 us -> 26.6 us  [exchange_y(): lax.all_to_all(value, 'chan', 0, 0, tiled=True, axis_index_groups=Y_GROUPS)]
    all_to_all x4, starting transfers between devices: 22.1 us -> 25 us  [exchange_y(): lax.all_to_all(value, 'chan', 0, 0, tiled=True, axis_index_groups=Y_GROUPS)]
  transfers between devices with their start and end apart: 9 -> 9, of which waited for: 7 -> 7; matrix products, arithmetic and copies ran while one was open for 3% -> 2% of each run, Pallas kernels for 9% -> 7%
where the time goes in v1:
time: 173 us; the launch traced here: 172 us
  waiting for transfers between devices  80.9 us (47%)
  Pallas kernels  47.9 us (28%)
  starting transfers between devices  37.4 us (22%)
  other arithmetic  3.74 us (2%)
  local copies, waits for them, and re-layouts  2 us (1%)
    ppermute x4, waiting for transfers between devices, swap_x(): return lax.ppermute(value, 'chan', X_PAIRS)  33.2 us
    pallas_call x1, Pallas kernels, body(): pl.pallas_call(spread_kernel, in_specs=[ANY], out_specs=ANY, out_shape=st...  27 us
    all_to_all x4, waiting for transfers between devices, exchange_y(): lax.all_to_all(value, 'chan', 0, 0, tiled=True, axis_index_groups=Y_GROUPS)  26.6 us
    all_to_all x4, starting transfers between devices, exchange_y(): lax.all_to_all(value, 'chan', 0, 0, tiled=True, axis_index_groups=Y_GROUPS)  25 us
    ppermute x1, waiting for transfers between devices, shifted(): lax.ppermute(value, axis, [(source, source + 1) for source in range(count...  21 us
    ppermute x4, starting transfers between devices, swap_x(): return lax.ppermute(value, 'chan', X_PAIRS)  10.5 us
    pallas_call x1, Pallas kernels, body(): pl.pallas_call(own_kernel, in_specs=[SCALAR, ANY, ANY, WHOLE], out_specs=...  4.73 us
    pallas_call x1, Pallas kernels, body(): pl.pallas_call(late_kernel, in_specs=[SCALAR, WHOLE, ANY, ANY], out_specs...  4.5 us
  transfers between devices with their start and end apart: 9, of which 7 were waited for; matrix products, arithmetic and copies ran while one was open for 2% of the time, Pallas kernels for 7%

profile of v1, /device:TPU:14, one launch (start us, length us, event | category | flops | bytes accessed | tf_op | source)
XLA Modules:
  0.0 172.2 jit_solution(18222994234770758217)
XLA Ops:
  0.0 27.0 %top.1 = bf16[8,208,256]{2,1,0:T(8,128)(2,1)} custom-call(bf16[320,256]{1,0:T(8,128)(2,1)} %rows_hbm.1), custom_call_target="tpu_custom_call" | custom-call | tf_op jit(solution)/shard_map/top/pallas_call | solution.py:269
  27.0 7.6 %all-to-all-start.1 = ((bf16[8,208,256]{2,1,0:T(8,128)(2,1)}), bf16[8,208,256]{2,1,0:T(8,128)(2,1)S(1)}, u32[]{:S(2)}, u32[]{:S(2)}) async-start(bf16[8,208,256]{2,1,0:T(8,128)(2,1)} %top.1), calls=%async_computation.1 | async-start | bytes 1703936 | tf_op jit(solution)/shard_map/all_to_all | solution.py:29
  34.6 0.8 slice_bitcast_fusion.1
  35.4 3.3 %collective-permute-start = (bf16[112,256]{1,0:T(8,128)(2,1)S(1)}, bf16[112,256]{1,0:T(8,128)(2,1)S(1)}, u32[]{:S(2)}, u32[]{:S(2)}) collective-permute-start(bf16[112,256]{1,0:T(8,128)(2,1)S(1)} %get-tuple-element.16), channel_id=1, source_target_pairs={{0,1},{1,0},{2,3},{3,2},{4,5},{5,4},{6,7},{7,6},{8,9},{9,8},{10,11... | collective-permute-start | bytes 172040 | tf_op jit(solution)/shard_map/ppermute | solution.py:25
  38.7 2.7 %collective-permute-done = bf16[112,256]{1,0:T(8,128)(2,1)S(1)} collective-permute-done((bf16[112,256]{1,0:T(8,128)(2,1)S(1)}, bf16[112,256]{1,0:T(8,128)(2,1)S(1)}, u32[]{:S(2)}, u32[]{:S(2)}) %collective-permute-start) | collective-permute-done | bytes 57376 | tf_op jit(solution)/shard_map/ppermute | solution.py:25
  41.5 0.0 copy-start.2
  41.5 17.6 %all-to-all-done.1.own_hbm = bf16[8,208,256]{2,1,0:T(8,128)(2,1)S(1)} async-done(((bf16[8,208,256]{2,1,0:T(8,128)(2,1)}), bf16[8,208,256]{2,1,0:T(8,128)(2,1)S(1)}, u32[]{:S(2)}, u32[]{:S(2)}) %all-to-all-start.1) | async-done | bytes 852000 | tf_op jit(solution)/shard_map/all_to_all | solution.py:29
  59.1 1.1 broadcast_in_dim.13
  60.1 3.6 %all-to-all-start = ((bf16[8,2,112,256]{3,2,1,0:T(8,128)(2,1)}), bf16[8,2,112,256]{3,2,1,0:T(8,128)(2,1)S(1)}, u32[]{:S(2)}, u32[]{:S(2)}) async-start(bf16[8,2,112,256]{3,2,1,0:T(8,128)(2,1)} %broadcast_in_dim.13), calls=%async_computation | async-start | bytes 1835008 | tf_op jit(solution)/shard_map/all_to_all | solution.py:29
  63.7 3.3 %collective-permute-start.1 = (bf16[8,208,256]{2,1,0:T(8,128)(2,1)S(1)}, bf16[8,208,256]{2,1,0:T(8,128)(2,1)S(1)}, u32[]{:S(2)}, u32[]{:S(2)}) collective-permute-start(bf16[8,208,256]{2,1,0:T(8,128)(2,1)S(1)} %all-to-all-done.1.own_hbm), channel_id=1, source_target_pairs={{0,1},{1,0},{2,3},{3,2},{4,5},{5,4},{6,7},{7,6},{8,9},{9,8},{10,11... | collective-permute-start | bytes 2555912 | tf_op jit(solution)/shard_map/ppermute | solution.py:25
  67.1 0.1 rev.4
  67.2 0.6 pad_convert_fusion.taps
  67.8 4.7 %own.1 = (f32[3,208,256]{2,1,0:T(8,128)}, f32[208,128]{1,0:T(8,128)}, bf16[256,256]{1,0:T(8,128)(2,1)}) custom-call(s32[1]{0:T(128)} %bitcast.x_ref, bf16[8,208,256]{2,1,0:T(8,128)(2,1)} %copy-done, bf16[3,8,2,256,256]{4,3,2,1,0:T(8,128)(2,1)} %bitcast.16, f32[16,256]{1,0:T(8,128)} %pad_convert_fusion.taps), custom_call_target="tpu_custom_call" | custom-call | tf_op jit(solution)/shard_map/own/pallas_call | solution.py:289
  72.5 13.9 %collective-permute-done.1.oth = bf16[8,208,256]{2,1,0:T(8,128)(2,1)S(1)} collective-permute-done((bf16[8,208,256]{2,1,0:T(8,128)(2,1)S(1)}, bf16[8,208,256]{2,1,0:T(8,128)(2,1)S(1)}, u32[]{:S(2)}, u32[]{:S(2)}) %collective-permute-start.1) | collective-permute-done | bytes 852000 | tf_op jit(solution)/shard_map/ppermute | solution.py:25
  86.5 3.8 %other.1.proj_hbm = bf16[208,768]{1,0:T(8,128)(2,1)} custom-call(s32[1]{0:T(128)} %bitcast.x_ref, bf16[8,208,256]{2,1,0:T(8,128)(2,1)S(1)} %collective-permute-done.1.oth, bf16[3,8,2,256,256]{4,3,2,1,0:T(8,128)(2,1)} %bitcast.17, f32[3,208,256]{2,1,0:T(8,128)} %get-tuple-element.10.sum_hbm, f32[208,128]{1,0:T(8,128)} %get-tuple-element.11.squares_hbm), custom_call_target="tpu_custom_call" | custom-call | tf_op jit(solution)/shard_map/other/pallas_call | solution.py:310
  90.3 4.5 %late.1.tail_hbm = bf16[136,768]{1,0:T(8,128)(2,1)} custom-call(s32[1]{0:T(128)} %bitcast.x_ref, bf16[8,2,112,256]{3,2,1,0:T(8,128)(2,1)S(1)} %all-to-all-done.pair2, bf16[3,8,2,256,256]{4,3,2,1,0:T(8,128)(2,1)} %bitcast.18, bf16[208,768]{1,0:T(8,128)(2,1)} %other.1.proj_hbm), custom_call_target="tpu_custom_call" | custom-call | tf_op jit(solution)/shard_map/late/pallas_call | solution.py:326
  94.8 4.0 %inner.1 = bf16[8,2,144,256]{3,2,1,0:T(8,128)(2,1)} custom-call(s32[1]{0:T(128)} %bitcast.x_ref, bf16[208,768]{1,0:T(8,128)(2,1)} %other.1.proj_hbm, bf16[136,768]{1,0:T(8,128)(2,1)} %late.1.tail_hbm, bf16[256,256]{1,0:T(8,128)(2,1)} %get-tuple-element.12.table_hbm, f32[3,3,256]{2,1,0:T(4,128)} %short.3, f32[1,256]{1,0:T(1,128)} %bitcast.20, ...), custom_call_target="tpu_custom_call" | custom-call | tf_op jit(solution)/shard_map/inner/pallas_call | solution.py:341
  98.7 7.0 %all-to-all-start.3 = ((bf16[8,2,144,256]{3,2,1,0:T(8,128)(2,1)}), bf16[8,2,144,256]{3,2,1,0:T(8,128)(2,1)S(1)}, u32[]{:S(2)}, u32[]{:S(2)}) async-start(bf16[8,2,144,256]{3,2,1,0:T(8,128)(2,1)} %inner.1), calls=%async_computation.3 | async-start | bytes 2359296 | tf_op jit(solution)/shard_map/all_to_all | solution.py:29
  105.7 1.9 %collective-permute-start.2 = (bf16[136,768]{1,0:T(8,128)(2,1)S(1)}, bf16[136,768]{1,0:T(8,128)(2,1)S(1)}, u32[]{:S(2)}, u32[]{:S(2)}) collective-permute-start(bf16[136,768]{1,0:T(8,128)(2,1)S(1)} %copy-done.1), channel_id=1, source_target_pairs={{0,16},{16,32},{32,48},{48,64},{64,80},{80,96},{96,112},{112,128},... | collective-permute-start | bytes 626696 | tf_op jit(solution)/shard_map/ppermute | solution.py:34
  107.6 21.0 %collective-permute-done.2.halo = bf16[136,768]{1,0:T(8,128)(2,1)S(1)} collective-permute-done((bf16[136,768]{1,0:T(8,128)(2,1)S(1)}, bf16[136,768]{1,0:T(8,128)(2,1)S(1)}, u32[]{:S(2)}, u32[]{:S(2)}) %collective-permute-start.2) | collective-permute-done | bytes 208928 | tf_op jit(solution)/shard_map/ppermute | solution.py:34
  128.7 4.0 %edge.1 = (bf16[8,176,256]{2,1,0:T(8,128)(2,1)}, bf16[8,176,256]{2,1,0:T(8,128)(2,1)}) custom-call(s32[1]{0:T(128)} %bitcast.x_ref, bf16[136,768]{1,0:T(8,128)(2,1)S(1)} %collective-permute-done.2.halo, bf16[208,768]{1,0:T(8,128)(2,1)} %other.1.proj_hbm, bf16[256,256]{1,0:T(8,128)(2,1)} %get-tuple-element.12.table_hbm, f32[3,3,256]{2,1,0:T(4,128)} %short.3, ...), custom_call_target="tpu_custom_call" | custom-call | tf_op jit(solution)/shard_map/edge/pallas_call | solution.py:364
  132.7 1.9 %collective-permute-start.3 = (bf16[8,176,256]{2,1,0:T(8,128)(2,1)}, bf16[8,176,256]{2,1,0:T(8,128)(2,1)S(1)}, u32[]{:S(2)}, u32[]{:S(2)}) collective-permute-start(bf16[8,176,256]{2,1,0:T(8,128)(2,1)} %get-tuple-element.14), channel_id=1, source_target_pairs={{0,1},{1,0},{2,3},{3,2},{4,5},{5,4},{6,7},{7,6},{8,9},{9,8},{10,11... | collective-permute-start | bytes 2162696 | tf_op jit(solution)/shard_map/ppermute | solution.py:25
  134.6 12.3 %collective-permute-done.3 = bf16[8,176,256]{2,1,0:T(8,128)(2,1)S(1)} collective-permute-done((bf16[8,176,256]{2,1,0:T(8,128)(2,1)}, bf16[8,176,256]{2,1,0:T(8,128)(2,1)S(1)}, u32[]{:S(2)}, u32[]{:S(2)}) %collective-permute-start.3) | collective-permute-done | bytes 720928 | tf_op jit(solution)/shard_map/ppermute | solution.py:25
  146.9 2.2 %add_convert_fusion = bf16[8,176,256]{2,1,0:T(8,128)(2,1)} fusion(bf16[8,176,256]{2,1,0:T(8,128)(2,1)S(1)} %collective-permute-done.3, bf16[8,176,256]{2,1,0:T(8,128)(2,1)} %get-tuple-element.13), kind=kLoop, calls=%fused_computation.1 | loop fusion | flops 1441792 | bytes 2162688 | tf_op jit(solution)/shard_map/convert_element_type | solution.py:389
  149.0 0.0 all-to-all-done.3
  149.0 6.9 %all-to-all-start.2 = ((bf16[8,176,256]{2,1,0:T(8,128)(2,1)}), bf16[8,176,256]{2,1,0:T(8,128)(2,1)S(1)}, u32[]{:S(2)}, u32[]{:S(2)}) async-start(bf16[8,176,256]{2,1,0:T(8,128)(2,1)} %add_convert_fusion), calls=%async_computation.2 | async-start | bytes 1441792 | tf_op jit(solution)/shard_map/all_to_all | solution.py:29
  156.0 0.2 convert_reduce_fusion
  156.1 1.9 %collective-permute-start.4 = (bf16[144,256]{1,0:T(8,128)(2,1)S(1)}, bf16[144,256]{1,0:T(8,128)(2,1)S(1)}, u32[]{:S(2)}, u32[]{:S(2)}) collective-permute-start(bf16[144,256]{1,0:T(8,128)(2,1)S(1)} %fusion.2), channel_id=1, source_target_pairs={{0,1},{1,0},{2,3},{3,2},{4,5},{5,4},{6,7},{7,6},{8,9},{9,8},{10,11... | collective-permute-start | bytes 221192 | tf_op jit(solution)/shard_map/ppermute | solution.py:25
  158.1 4.3 %collective-permute-done.4 = bf16[144,256]{1,0:T(8,128)(2,1)S(1)} collective-permute-done((bf16[144,256]{1,0:T(8,128)(2,1)S(1)}, bf16[144,256]{1,0:T(8,128)(2,1)S(1)}, u32[]{:S(2)}, u32[]{:S(2)}) %collective-permute-start.4) | collective-permute-done | bytes 73760 | tf_op jit(solution)/shard_map/ppermute | solution.py:25
  162.4 9.0 %all-to-all-done.2 = bf16[8,176,256]{2,1,0:T(8,128)(2,1)S(1)} async-done(((bf16[8,176,256]{2,1,0:T(8,128)(2,1)}), bf16[8,176,256]{2,1,0:T(8,128)(2,1)S(1)}, u32[]{:S(2)}, u32[]{:S(2)}) %all-to-all-start.2) | async-done | bytes 720928 | tf_op jit(solution)/shard_map/all_to_all | solution.py:29
  171.4 0.1 reduce_sum.21
  171.5 0.7 pad_maximum_fusion
  (9 shorter events, 0.1 us)
Async XLA Ops:
  27.0 32.1 %all-to-all-start.1 = ((bf16[8,208,256]{2,1,0:T(8,128)(2,1)}), bf16[8,208,256]{2,1,0:T(8,128)(2,1)S(1)}, u32[]{:S(2)}, u32[]{:S(2)}) async-start(bf16[8,208,256]{2,1,0:T(8,128)(2,1)} %top.1), calls=%async_computation.1 | async-start | bytes 1703936 | tf_op jit(solution)/shard_map/all_to_all | solution.py:29
  35.4 6.1 %collective-permute-start = (bf16[112,256]{1,0:T(8,128)(2,1)S(1)}, bf16[112,256]{1,0:T(8,128)(2,1)S(1)}, u32[]{:S(2)}, u32[]{:S(2)}) collective-permute-start(bf16[112,256]{1,0:T(8,128)(2,1)S(1)} %get-tuple-element.16), channel_id=1, source_target_pairs={{0,1},{1,0},{2,3},{3,2},{4,5},{5,4},{6,7},{7,6},{8,9},{9,8},{10,11... | collective-permute-start | bytes 172040 | tf_op jit(solution)/shard_map/ppermute | solution.py:25
  41.5 25.6 %copy-start.2 = (bf16[16,128]{1,0:T(8,128)(2,1)S(1)}, bf16[16,128]{1,0:T(8,128)(2,1)}, u32[]{:S(2)}) copy-start(bf16[16,128]{1,0:T(8,128)(2,1)} %param.9) | copy-start | bytes 12292
  59.1 8.0 %copy-start = (bf16[8,208,256]{2,1,0:T(8,128)(2,1)}, bf16[8,208,256]{2,1,0:T(8,128)(2,1)S(1)}, u32[]{:S(2)}) copy-start(bf16[8,208,256]{2,1,0:T(8,128)(2,1)S(1)} %all-to-all-done.1.own_hbm) | copy-start | bytes 2555908
  60.1 30.1 %all-to-all-start = ((bf16[8,2,112,256]{3,2,1,0:T(8,128)(2,1)}), bf16[8,2,112,256]{3,2,1,0:T(8,128)(2,1)S(1)}, u32[]{:S(2)}, u32[]{:S(2)}) async-start(bf16[8,2,112,256]{3,2,1,0:T(8,128)(2,1)} %broadcast_in_dim.13), calls=%async_computation | async-start | bytes 1835008 | tf_op jit(solution)/shard_map/all_to_all | solution.py:29
  63.7 22.8 %collective-permute-start.1 = (bf16[8,208,256]{2,1,0:T(8,128)(2,1)S(1)}, bf16[8,208,256]{2,1,0:T(8,128)(2,1)S(1)}, u32[]{:S(2)}, u32[]{:S(2)}) collective-permute-start(bf16[8,208,256]{2,1,0:T(8,128)(2,1)S(1)} %all-to-all-done.1.own_hbm), channel_id=1, source_target_pairs={{0,1},{1,0},{2,3},{3,2},{4,5},{5,4},{6,7},{7,6},{8,9},{9,8},{10,11... | collective-permute-start | bytes 2555912 | tf_op jit(solution)/shard_map/ppermute | solution.py:25
  98.7 7.0 %copy-start.1 = (bf16[136,768]{1,0:T(8,128)(2,1)S(1)}, bf16[136,768]{1,0:T(8,128)(2,1)}, u32[]{:S(2)}) copy-start(bf16[136,768]{1,0:T(8,128)(2,1)} %late.1.tail_hbm) | copy-start | bytes 626692
  98.7 50.3 %all-to-all-start.3 = ((bf16[8,2,144,256]{3,2,1,0:T(8,128)(2,1)}), bf16[8,2,144,256]{3,2,1,0:T(8,128)(2,1)S(1)}, u32[]{:S(2)}, u32[]{:S(2)}) async-start(bf16[8,2,144,256]{3,2,1,0:T(8,128)(2,1)} %inner.1), calls=%async_computation.3 | async-start | bytes 2359296 | tf_op jit(solution)/shard_map/all_to_all | solution.py:29
  105.7 23.0 %collective-permute-start.2 = (bf16[136,768]{1,0:T(8,128)(2,1)S(1)}, bf16[136,768]{1,0:T(8,128)(2,1)S(1)}, u32[]{:S(2)}, u32[]{:S(2)}) collective-permute-start(bf16[136,768]{1,0:T(8,128)(2,1)S(1)} %copy-done.1), channel_id=1, source_target_pairs={{0,16},{16,32},{32,48},{48,64},{64,80},{80,96},{96,112},{112,128},... | collective-permute-start | bytes 626696 | tf_op jit(solution)/shard_map/ppermute | solution.py:34
  132.7 14.2 %collective-permute-start.3 = (bf16[8,176,256]{2,1,0:T(8,128)(2,1)}, bf16[8,176,256]{2,1,0:T(8,128)(2,1)S(1)}, u32[]{:S(2)}, u32[]{:S(2)}) collective-permute-start(bf16[8,176,256]{2,1,0:T(8,128)(2,1)} %get-tuple-element.14), channel_id=1, source_target_pairs={{0,1},{1,0},{2,3},{3,2},{4,5},{5,4},{6,7},{7,6},{8,9},{9,8},{10,11... | collective-permute-start | bytes 2162696 | tf_op jit(solution)/shard_map/ppermute | solution.py:25
  149.0 22.4 %all-to-all-start.2 = ((bf16[8,176,256]{2,1,0:T(8,128)(2,1)}), bf16[8,176,256]{2,1,0:T(8,128)(2,1)S(1)}, u32[]{:S(2)}, u32[]{:S(2)}) async-start(bf16[8,176,256]{2,1,0:T(8,128)(2,1)} %add_convert_fusion), calls=%async_computation.2 | async-start | bytes 1441792 | tf_op jit(solution)/shard_map/all_to_all | solution.py:29
  156.1 6.2 %collective-permute-start.4 = (bf16[144,256]{1,0:T(8,128)(2,1)S(1)}, bf16[144,256]{1,0:T(8,128)(2,1)S(1)}, u32[]{:S(2)}, u32[]{:S(2)}) collective-permute-start(bf16[144,256]{1,0:T(8,128)(2,1)S(1)} %fusion.2), channel_id=1, source_target_pairs={{0,1},{1,0},{2,3},{3,2},{4,5},{5,4},{6,7},{7,6},{8,9},{9,8},{10,11... | collective-permute-start | bytes 221192 | tf_op jit(solution)/shard_map/ppermute | solution.py:25

commit v2 on v1

--- a/solution.py
+++ b/solution.py
@@ -8,8 +8,8 @@
 
 YS = 8
 XS = 2
-LATE_IN = 112
-LATE_OUT = 144
+LATE_IN = 128
+LATE_OUT = 160
 BLOCK = 16
 HALO = 136
 WIDE_FROM = 320 - LATE_OUT - 128 - 16
@@ -71,13 +71,30 @@
         copy.wait()
 
 
-def spread_kernel(rows_hbm, out_hbm, sent):
-    copies = [
-        pltpu.make_async_copy(rows_hbm.at[0 : out_hbm.shape[1]], out_hbm.at[y], sent.at[y])
-        for y in range(YS)
-    ]
+def spread_kernel(rows_hbm, out_hbm, rows, sent):
+    fetch = pltpu.make_async_copy(rows_hbm.at[0 : rows.shape[0]], rows, sent.at[YS])
+    fetch.start()
+    fetch.wait()
+    copies = [pltpu.make_async_copy(rows, out_hbm.at[y], sent.at[y]) for y in range(YS)]
     start_all(copies)
     wait_all(copies)
+
+
+def slab_kernel(x_ref, weight_hbm, out_hbm, slab, arrived, sent):
+    other = 1 - x_ref[0]
+    fetches = []
+    sends = []
+    for y in range(YS):
+        first = pl.multiple_of(y * 512 + other * 256, 256)
+        fetches.append(
+            pltpu.make_async_copy(weight_hbm.at[:, pl.ds(first, 256)], slab.at[y], arrived.at[y])
+        )
+        sends.append(pltpu.make_async_copy(slab.at[y], out_hbm.at[y], sent.at[y]))
+    start_all(fetches)
+    for y in range(YS):
+        fetches[y].wait()
+        sends[y].start()
+    wait_all(sends)
 
 
 def own_kernel(
@@ -177,72 +194,65 @@
         mixed[BLOCK * b : BLOCK * b + BLOCK] = (queries * total).astype(BF16)
 
 
-def out_rows(x, value, weight, store):
-    for y in range(YS):
-        mine = pl.multiple_of(y * 512 + x * 256, 256)
-        other = pl.multiple_of(y * 512 + 256 - x * 256, 256)
-        store(y, 0, jnp.dot(value, weight[:, pl.ds(mine, 256)], preferred_element_type=F32).astype(BF16))
-        store(y, 1, jnp.dot(value, weight[:, pl.ds(other, 256)], preferred_element_type=F32).astype(BF16))
-
-
 def inner_kernel(
-    x_ref, proj_hbm, tail_hbm, table_hbm, short, skip, out_hbm, pair_hbm,
-    proj1, tail, table, out_weight, wide, gated, mixed, pair, arrived, sent
+    proj_hbm, tail_hbm, table_hbm, short, skip, mixed_hbm,
+    proj1, tail, table, wide, gated, mixed, arrived
 ):
     proj_fetch = pltpu.make_async_copy(proj_hbm.at[WIDE_FROM:], proj1, arrived.at[0])
     tail_fetch = pltpu.make_async_copy(tail_hbm.at[HALO - LATE_IN :], tail, arrived.at[1])
     table_fetch = pltpu.make_async_copy(table_hbm, table, arrived.at[2])
-    out_fetch = pltpu.make_async_copy(out_hbm, out_weight, arrived.at[3])
-    start_all([proj_fetch, tail_fetch, table_fetch, out_fetch])
+    start_all([proj_fetch, tail_fetch, table_fetch])
     count = proj1.shape[0]
     proj_fetch.wait()
     wide[0:count] = proj1[...].astype(F32)
     tail_fetch.wait()
     wide[count:] = tail[...].astype(F32)
     table_fetch.wait()
-    mix_rows(wide, 16, gated, table, short, skip, mixed, LATE_OUT)
-    out_fetch.wait()
-    sends = [pltpu.make_async_copy(pair.at[y], pair_hbm.at[y], sent.at[y]) for y in range(YS)]
-
-    def place(y, side, value):
-        pair[y, side] = value
-        if side == 1:
-            sends[y].start()
-
-    out_rows(x_ref[0], mixed[...], out_weight, place)
-    wait_all(sends)
+    mix_rows(wide, 16, gated, table, short, skip, mixed, mixed.shape[0])
+    send = pltpu.make_async_copy(mixed, mixed_hbm, arrived.at[3])
+    send.start()
+    send.wait()
 
 
 def edge_kernel(
-    x_ref, halo, proj_hbm, table_hbm, short, skip, out_hbm, send_hbm, keep_hbm,
-    proj1, table, out_weight, wide, gated, mixed, send, keep, arrived, sent
+    halo, proj_hbm, table_hbm, short, skip, mixed_hbm, proj1, table, wide, gated, mixed, arrived
 ):
     count = mixed.shape[0]
     proj_fetch = pltpu.make_async_copy(proj_hbm.at[0:count], proj1, arrived.at[0])
     table_fetch = pltpu.make_async_copy(table_hbm, table, arrived.at[1])
-    out_fetch = pltpu.make_async_copy(out_hbm, out_weight, arrived.at[2])
-    for fetch in (proj_fetch, table_fetch, out_fetch):
-        fetch.start()
+    start_all([proj_fetch, table_fetch])
     wide[0:HALO] = halo[...].astype(F32)
     proj_fetch.wait()
     wide[HALO:] = proj1[...].astype(F32)
     table_fetch.wait()
     mix_rows(wide, HALO - 128, gated, table, short, skip, mixed, count)
-    out_fetch.wait()
-
-    sends = [pltpu.make_async_copy(send.at[y], send_hbm.at[y], sent.at[y]) for y in range(YS)]
-    keeps = [pltpu.make_async_copy(keep.at[y], keep_hbm.at[y], sent.at[YS + y]) for y in range(YS)]
-
-    def place(y, side, value):
-        if side == 0:
-            keep[y] = value
-            keeps[y].start()
-        else:
-            send[y] = value
-            sends[y].start()
-
-    out_rows(x_ref[0], mixed[...], out_weight, place)
-    wait_all(sends + keeps)
+    send = pltpu.make_async_copy(mixed, mixed_hbm, arrived.at[2])
+    send.start()
+    send.wait()
+
+
+def sums_kernel(x_ref, own_hbm, oth, weight_hbm, slab_hbm, out_hbm, own, weight, slab, out, arrived, sent):
+    x = x_ref[0]
+    own_fetch = pltpu.make_async_copy(own_hbm, own, arrived.at[2 * YS])
+    own_fetch.start()
+    fetches = []
+    sends = []
+    for y in range(YS):
+        first = pl.multiple_of(y * 512 + x * 256, 256)
+        fetches.append(
+            pltpu.make_async_copy(weight_hbm.at[:, pl.ds(first, 256)], weight.at[y], arrived.at[y])
+        )
+        fetches.append(pltpu.make_async_copy(slab_hbm.at[y], slab.at[y], arrived.at[YS + y]))
+        sends.append(pltpu.make_async_copy(out.at[y], out_hbm.at[y], sent.at[y]))
+    start_all(fetches)
+    own_fetch.wait()
+    for y in range(YS):
+        wait_all(fetches[2 * y : 2 * y + 2])
+        total = jnp.dot(own[...], weight[y], preferred_element_type=F32)
+        total = total + jnp.dot(oth[...], slab[y], preferred_element_type=F32)
+        out[y] = total.astype(BF16)
+        sends[y].start()
+    wait_all(sends)
 
 
 WHOLE = pl.BlockSpec(memory_space=VMEM)
@@ -271,11 +281,22 @@
         in_specs=[ANY],
         out_specs=ANY,
         out_shape=struct(YS, early_in, 256),
-        scratch_shapes=[copies((YS,))],
+        scratch_shapes=[VMEM((early_in, 256), BF16), copies((YS + 1,))],
         compiler_params=PARAMS,
         name="top",
     )(tokens)
     tail_other = swap_x(tail)
+    slab_shape = (YS, 256, 256)
+    slab = pl.pallas_call(
+        slab_kernel,
+        in_specs=[SCALAR, ANY],
+        out_specs=ANY,
+        out_shape=struct(*slab_shape),
+        scratch_shapes=[VMEM(slab_shape, BF16), copies((YS,)), copies((YS,))],
+        compiler_params=PARAMS,
+        name="slab",
+    )(x, out_weight)
+    slab = swap_x(slab)
     own1 = exchange_y(top)
     oth1 = swap_x(own1)
     both = jnp.stack([tail, tail_other])
@@ -284,7 +305,6 @@
 
     half_space = VMEM((3, YS, 256, 256), BF16)
     table_space = VMEM((16 * BLOCK, 256), BF16)
-    out_space = VMEM(out_weight.shape, BF16)
     sum_shape = (3, early_in, 256)
     sums, squares, table = pl.pallas_call(
         own_kernel,
@@ -338,59 +358,68 @@
         compiler_params=PARAMS,
         name="late",
     )(x, in_vmem(pair2), weight, proj1)
-    pair = pl.pallas_call(
+    late_mixed = pl.pallas_call(
         inner_kernel,
-        in_specs=[SCALAR, ANY, ANY, ANY, WHOLE, WHOLE, ANY],
-        out_specs=ANY,
-        out_shape=struct(YS, 2, LATE_OUT, 256),
+        in_specs=[ANY, ANY, ANY, WHOLE, WHOLE],
+        out_specs=ANY,
+        out_shape=struct(LATE_OUT, 256),
         scratch_shapes=[
             VMEM((early_in - WIDE_FROM, 768), BF16),
             VMEM((LATE_IN, 768), BF16),
             table_space,
-            out_space,
             VMEM((rows - WIDE_FROM, 768), F32),
             VMEM((LATE_OUT + 256, 256), BF16),
             VMEM((LATE_OUT, 256), BF16),
-            VMEM((YS, 2, LATE_OUT, 256), BF16),
             copies((4,)),
-            copies((YS,)),
         ],
         compiler_params=PARAMS,
         name="inner",
-    )(x, proj1, tail_rows, table, short_filter, skip, out_weight)
+    )(proj1, tail_rows, table, short_filter, skip)
+
+    def column_sums(own, oth):
+        count = own.shape[0]
+        return pl.pallas_call(
+            sums_kernel,
+            in_specs=[SCALAR, ANY, WHOLE, ANY, ANY],
+            out_specs=ANY,
+            out_shape=struct(YS, count, 256),
+            scratch_shapes=[
+                VMEM((count, 256), BF16),
+                VMEM(slab_shape, BF16),
+                VMEM(slab_shape, BF16),
+                VMEM((YS, count, 256), BF16),
+                copies((2 * YS + 1,)),
+                copies((YS,)),
+            ],
+            compiler_params=PARAMS,
+        )(x, own, in_vmem(oth), out_weight, slab)
 
     halo = shifted(tail_rows, "seq")
-    pair = exchange_y(pair)
-    send, keep = pl.pallas_call(
+    late_other = swap_x(late_mixed)
+    late_sums = column_sums(late_mixed, late_other)
+    late_sums = exchange_y(late_sums)
+    edge_mixed = pl.pallas_call(
         edge_kernel,
-        in_specs=[SCALAR, WHOLE, ANY, ANY, WHOLE, WHOLE, ANY],
-        out_specs=[ANY] * 2,
-        out_shape=[struct(YS, early_out, 256), struct(YS, early_out, 256)],
+        in_specs=[WHOLE, ANY, ANY, WHOLE, WHOLE],
+        out_specs=ANY,
+        out_shape=struct(early_out, 256),
         scratch_shapes=[
             VMEM((early_out, 768), BF16),
             table_space,
-            out_space,
             VMEM((HALO + early_out, 768), F32),
             VMEM((early_out + 256, 256), BF16),
             VMEM((early_out, 256), BF16),
-            VMEM((YS, early_out, 256), BF16),
-            VMEM((YS, early_out, 256), BF16),
             copies((3,)),
-            copies((2 * YS,)),
         ],
         compiler_params=PARAMS,
         name="edge",
-    )(x, in_vmem(halo), proj1, table, short_filter, skip, out_weight)
-
-    received = swap_x(send)
-    sums = jnp.sum(pair.astype(F32), axis=0)
-    late_send = sums[1].astype(BF16)
-    late_received = swap_x(late_send)
-    merged = (keep.astype(F32) + received.astype(F32)).astype(BF16)
-    merged = exchange_y(merged)
-    early_sum = jnp.sum(merged.astype(F32), axis=0).astype(BF16)
-    late_sum = (sums[0] + late_received.astype(F32)).astype(BF16)
-    return jnp.concatenate([early_sum, late_sum], axis=0)
+    )(in_vmem(halo), proj1, table, short_filter, skip)
+    edge_other = swap_x(edge_mixed)
+    edge_sums = column_sums(edge_mixed, edge_other)
+    edge_sums = exchange_y(edge_sums)
+    late_total = jnp.sum(late_sums.astype(F32), axis=0).astype(BF16)
+    edge_total = jnp.sum(edge_sums.astype(F32), axis=0).astype(BF16)
+    return jnp.concatenate([edge_total, late_total], axis=0)
 
 
 def solution(mesh):

time: 173 us -> 171 us (0.988)
  Pallas kernels: 47.9 us -> 30.4 us
  waiting for transfers between devices: 80.9 us -> 94.4 us
  starting transfers between devices: 37.4 us -> 41.3 us
  other arithmetic: 3.74 us -> 1.48 us
    pallas_call x1, Pallas kernels: 27 us -> 1.88 us  [body(): pl.pallas_call(spread_kernel, in_specs=[ANY], out_specs=ANY, out_shape=st...]
    ppermute x4 -> x5, waiting for transfers between devices: 33.2 us -> 43.5 us  [swap_x(): return lax.ppermute(value, 'chan', X_PAIRS)]
    pallas_call x2 -> x5, Pallas kernels: 7.95 us -> 15.8 us  [the longest x2 7.49 us: column_sums(): pl.pallas_call(sums_kernel, in_specs=[SCALAR, ANY, WHOLE, ANY, ANY], out_...]
    all_to_all x4, waiting for transfers between devices: 26.6 us -> 30.7 us  [exchange_y(): lax.all_to_all(value, 'chan', 0, 0, tiled=True, axis_index_groups=Y_GROUPS)]
    ppermute x4 -> x5, starting transfers between devices: 10.5 us -> 14.4 us  [swap_x(): return lax.ppermute(value, 'chan', X_PAIRS)]
    convert_element_type x2 -> x0, other arithmetic: 2.18 us -> none  [the longest x1 2.16 us: body(): merged = (keep.astype(F32) + received.astype(F32)).astype(BF16)]
  transfers between devices with their start and end apart: 9 -> 10, of which waited for: 7 -> 7; matrix products, arithmetic and copies ran while one was open for 2% -> 1% of each run, Pallas kernels for 7% -> 15%
where the time goes in v2:
time: 171 us; the launch traced here: 170 us
  waiting for transfers between devices  94.4 us (55%)
  starting transfers between devices  41.3 us (24%)
  Pallas kernels  30.4 us (18%)
  local copies, waits for them, and re-layouts  2.24 us (1%)
    ppermute x5, waiting for transfers between devices, swap_x(): return lax.ppermute(value, 'chan', X_PAIRS)  43.5 us
    all_to_all x4, waiting for transfers between devices, exchange_y(): lax.all_to_all(value, 'chan', 0, 0, tiled=True, axis_index_groups=Y_GROUPS)  30.7 us
    all_to_all x4, starting transfers between devices, exchange_y(): lax.all_to_all(value, 'chan', 0, 0, tiled=True, axis_index_groups=Y_GROUPS)  24.9 us
    ppermute x1, waiting for transfers between devices, shifted(): lax.ppermute(value, axis, [(source, source + 1) for source in range(count...  20.2 us
    ppermute x5, starting transfers between devices, swap_x(): return lax.ppermute(value, 'chan', X_PAIRS)  14.4 us
    pallas_call x2, Pallas kernels, column_sums(): pl.pallas_call(sums_kernel, in_specs=[SCALAR, ANY, WHOLE, ANY, ANY], out_...  7.49 us
    pallas_call x1, Pallas kernels, body(): pl.pallas_call(own_kernel, in_specs=[SCALAR, ANY, ANY, WHOLE], out_specs=...  4.61 us
    pallas_call x1, Pallas kernels, body(): pl.pallas_call(late_kernel, in_specs=[SCALAR, WHOLE, ANY, ANY], out_specs...  4.52 us
  transfers between devices with their start and end apart: 10, of which 7 were waited for; matrix products, arithmetic and copies ran while one was open for 1% of the time, Pallas kernels for 15%

profile of v2, /device:TPU:14, one launch (start us, length us, event | category | flops | bytes accessed | tf_op | source)
XLA Modules:
  0.0 170.0 jit_solution(14787647297653077059)
XLA Ops:
  0.0 1.9 %top.1 = bf16[8,192,256]{2,1,0:T(8,128)(2,1)} custom-call(bf16[320,256]{1,0:T(8,128)(2,1)} %rows_hbm.1), custom_call_target="tpu_custom_call" | custom-call | tf_op jit(solution)/shard_map/top/pallas_call | solution.py:279
  1.9 7.6 %all-to-all-start.1 = ((bf16[8,192,256]{2,1,0:T(8,128)(2,1)}), bf16[8,192,256]{2,1,0:T(8,128)(2,1)S(1)}, u32[]{:S(2)}, u32[]{:S(2)}) async-start(bf16[8,192,256]{2,1,0:T(8,128)(2,1)} %top.1), calls=%async_computation.1 | async-start | bytes 1572864 | tf_op jit(solution)/shard_map/all_to_all | solution.py:29
  9.5 0.8 slice_bitcast_fusion
  10.3 3.3 %collective-permute-start = (bf16[128,256]{1,0:T(8,128)(2,1)S(1)}, bf16[128,256]{1,0:T(8,128)(2,1)S(1)}, u32[]{:S(2)}, u32[]{:S(2)}) collective-permute-start(bf16[128,256]{1,0:T(8,128)(2,1)S(1)} %get-tuple-element.12), channel_id=1, source_target_pairs={{0,1},{1,0},{2,3},{3,2},{4,5},{5,4},{6,7},{7,6},{8,9},{9,8},{10,11... | collective-permute-start | bytes 196616 | tf_op jit(solution)/shard_map/ppermute | solution.py:25
  13.7 2.8 %collective-permute-done = bf16[128,256]{1,0:T(8,128)(2,1)S(1)} collective-permute-done((bf16[128,256]{1,0:T(8,128)(2,1)S(1)}, bf16[128,256]{1,0:T(8,128)(2,1)S(1)}, u32[]{:S(2)}, u32[]{:S(2)}) %collective-permute-start) | collective-permute-done | bytes 65568 | tf_op jit(solution)/shard_map/ppermute | solution.py:25
  16.5 16.1 %all-to-all-done.1.own_hbm = bf16[8,192,256]{2,1,0:T(8,128)(2,1)S(1)} async-done(((bf16[8,192,256]{2,1,0:T(8,128)(2,1)}), bf16[8,192,256]{2,1,0:T(8,128)(2,1)S(1)}, u32[]{:S(2)}, u32[]{:S(2)}) %all-to-all-start.1) | async-done | bytes 786464 | tf_op jit(solution)/shard_map/all_to_all | solution.py:29
  32.6 1.2 broadcast_in_dim.13
  33.8 0.1 copy-done.1
  33.9 3.6 %all-to-all-start = ((bf16[8,2,128,256]{3,2,1,0:T(8,128)(2,1)}), bf16[8,2,128,256]{3,2,1,0:T(8,128)(2,1)S(1)}, u32[]{:S(2)}, u32[]{:S(2)}) async-start(bf16[8,2,128,256]{3,2,1,0:T(8,128)(2,1)} %broadcast_in_dim.13), calls=%async_computation | async-start | bytes 2097152 | tf_op jit(solution)/shard_map/all_to_all | solution.py:29
  37.4 2.1 %slab.1 = bf16[8,256,256]{2,1,0:T(8,128)(2,1)} custom-call(s32[1]{0:T(128)} %bitcast.x_ref, bf16[256,4096]{1,0:T(8,128)(2,1)} %weight_hbm.5), custom_call_target="tpu_custom_call" | custom-call | tf_op jit(solution)/shard_map/slab/pallas_call | solution.py:290
  39.6 3.3 %collective-permute-start.4 = (bf16[8,256,256]{2,1,0:T(8,128)(2,1)}, bf16[8,256,256]{2,1,0:T(8,128)(2,1)S(1)}, u32[]{:S(2)}, u32[]{:S(2)}) collective-permute-start(bf16[8,256,256]{2,1,0:T(8,128)(2,1)} %slab.1), channel_id=1, source_target_pairs={{0,1},{1,0},{2,3},{3,2},{4,5},{5,4},{6,7},{7,6},{8,9},{9,8},{10,11... | collective-permute-start | bytes 3145736 | tf_op jit(solution)/shard_map/ppermute | solution.py:25
  42.9 2.5 %collective-permute-start.1 = (bf16[8,192,256]{2,1,0:T(8,128)(2,1)}, bf16[8,192,256]{2,1,0:T(8,128)(2,1)S(1)}, u32[]{:S(2)}, u32[]{:S(2)}) collective-permute-start(bf16[8,192,256]{2,1,0:T(8,128)(2,1)} %copy-done.1), channel_id=1, source_target_pairs={{0,1},{1,0},{2,3},{3,2},{4,5},{5,4},{6,7},{7,6},{8,9},{9,8},{10,11... | collective-permute-start | bytes 2359304 | tf_op jit(solution)/shard_map/ppermute | solution.py:25
  45.5 0.6 pad_convert_fusion.taps
  46.1 4.6 %own.1 = (f32[3,192,256]{2,1,0:T(8,128)}, f32[192,128]{1,0:T(8,128)}, bf16[256,256]{1,0:T(8,128)(2,1)}) custom-call(s32[1]{0:T(128)} %bitcast.x_ref, bf16[8,192,256]{2,1,0:T(8,128)(2,1)} %copy-done.1, bf16[3,8,2,256,256]{4,3,2,1,0:T(8,128)(2,1)} %bitcast.8, f32[16,256]{1,0:T(8,128)} %pad_convert_fusion.taps), custom_call_target="tpu_custom_call" | custom-call | tf_op jit(solution)/shard_map/own/pallas_call | solution.py:309
  50.7 32.9 %collective-permute-done.1.oth = bf16[8,192,256]{2,1,0:T(8,128)(2,1)S(1)} collective-permute-done((bf16[8,192,256]{2,1,0:T(8,128)(2,1)}, bf16[8,192,256]{2,1,0:T(8,128)(2,1)S(1)}, u32[]{:S(2)}, u32[]{:S(2)}) %collective-permute-start.1) | collective-permute-done | bytes 786464 | tf_op jit(solution)/shard_map/ppermute | solution.py:25
  83.6 3.7 %other.1.proj_hbm = bf16[192,768]{1,0:T(8,128)(2,1)} custom-call(s32[1]{0:T(128)} %bitcast.x_ref, bf16[8,192,256]{2,1,0:T(8,128)(2,1)S(1)} %collective-permute-done.1.oth, bf16[3,8,2,256,256]{4,3,2,1,0:T(8,128)(2,1)} %bitcast.9, f32[3,192,256]{2,1,0:T(8,128)} %get-tuple-element.8.sum_hbm, f32[192,128]{1,0:T(8,128)} %get-tuple-element.9.squares_hbm), custom_call_target="tpu_custom_call" | custom-call | tf_op jit(solution)/shard_map/other/pallas_call | solution.py:330
  87.3 4.5 %late.1.tail_hbm = bf16[136,768]{1,0:T(8,128)(2,1)} custom-call(s32[1]{0:T(128)} %bitcast.x_ref, bf16[8,2,128,256]{3,2,1,0:T(8,128)(2,1)S(1)} %all-to-all-done.pair2, bf16[3,8,2,256,256]{4,3,2,1,0:T(8,128)(2,1)} %bitcast.10, bf16[192,768]{1,0:T(8,128)(2,1)} %other.1.proj_hbm), custom_call_target="tpu_custom_call" | custom-call | tf_op jit(solution)/shard_map/late/pallas_call | solution.py:346
  91.8 3.1 %inner.1.own_hbm = bf16[160,256]{1,0:T(8,128)(2,1)} custom-call(bf16[192,768]{1,0:T(8,128)(2,1)} %other.1.proj_hbm, bf16[136,768]{1,0:T(8,128)(2,1)} %late.1.tail_hbm, bf16[256,256]{1,0:T(8,128)(2,1)} %get-tuple-element.10.table_hbm, f32[3,3,256]{2,1,0:T(4,128)} %short.3, f32[1,256]{1,0:T(1,128)} %bitcast.12), custom_call_target="tpu_custom_call" | custom-call | tf_op jit(solution)/shard_map/inner/pallas_call | solution.py:361
  94.9 3.3 %collective-permute-start.5 = (bf16[160,256]{1,0:T(8,128)(2,1)}, bf16[160,256]{1,0:T(8,128)(2,1)S(1)}, u32[]{:S(2)}, u32[]{:S(2)}) collective-permute-start(bf16[160,256]{1,0:T(8,128)(2,1)} %inner.1.own_hbm), channel_id=1, source_target_pairs={{0,1},{1,0},{2,3},{3,2},{4,5},{5,4},{6,7},{7,6},{8,9},{9,8},{10,11... | collective-permute-start | bytes 245768 | tf_op jit(solution)/shard_map/ppermute | solution.py:25
  98.3 3.2 %collective-permute-done.5.oth = bf16[160,256]{1,0:T(8,128)(2,1)S(1)} collective-permute-done((bf16[160,256]{1,0:T(8,128)(2,1)}, bf16[160,256]{1,0:T(8,128)(2,1)S(1)}, u32[]{:S(2)}, u32[]{:S(2)}) %collective-permute-start.5) | collective-permute-done | bytes 81952 | tf_op jit(solution)/shard_map/ppermute | solution.py:25
  101.5 3.7 %shard_map.65 = bf16[8,160,256]{2,1,0:T(8,128)(2,1)} custom-call(s32[1]{0:T(128)} %bitcast.x_ref, bf16[160,256]{1,0:T(8,128)(2,1)} %inner.1.own_hbm, bf16[160,256]{1,0:T(8,128)(2,1)S(1)} %collective-permute-done.5.oth, bf16[256,4096]{1,0:T(8,128)(2,1)} %weight_hbm.5, bf16[8,256,256]{2,1,0:T(8,128)(2,1)} %copy-done), custom_call_target="tpu_custom_call" | custom-call | tf_op jit(solution)/shard_map/pallas_call | solution.py:381
  105.2 6.8 %all-to-all-start.3 = ((bf16[8,160,256]{2,1,0:T(8,128)(2,1)}), bf16[8,160,256]{2,1,0:T(8,128)(2,1)S(1)}, u32[]{:S(2)}, u32[]{:S(2)}) async-start(bf16[8,160,256]{2,1,0:T(8,128)(2,1)} %shard_map.65), calls=%async_computation.3 | async-start | bytes 1310720 | tf_op jit(solution)/shard_map/all_to_all | solution.py:29
  112.1 1.9 %collective-permute-start.2 = (bf16[136,768]{1,0:T(8,128)(2,1)}, bf16[136,768]{1,0:T(8,128)(2,1)S(1)}, u32[]{:S(2)}, u32[]{:S(2)}) collective-permute-start(bf16[136,768]{1,0:T(8,128)(2,1)} %late.1.tail_hbm), channel_id=1, source_target_pairs={{0,16},{16,32},{32,48},{48,64},{64,80},{80,96},{96,112},{112,128},... | collective-permute-start | bytes 626696 | tf_op jit(solution)/shard_map/ppermute | solution.py:34
  114.0 20.2 %collective-permute-done.2.halo = bf16[136,768]{1,0:T(8,128)(2,1)S(1)} collective-permute-done((bf16[136,768]{1,0:T(8,128)(2,1)}, bf16[136,768]{1,0:T(8,128)(2,1)S(1)}, u32[]{:S(2)}, u32[]{:S(2)}) %collective-permute-start.2) | collective-permute-done | bytes 208928 | tf_op jit(solution)/shard_map/ppermute | solution.py:34
  134.2 3.1 %edge.1.own_hbm = bf16[160,256]{1,0:T(8,128)(2,1)} custom-call(bf16[136,768]{1,0:T(8,128)(2,1)S(1)} %collective-permute-done.2.halo, bf16[192,768]{1,0:T(8,128)(2,1)} %other.1.proj_hbm, bf16[256,256]{1,0:T(8,128)(2,1)} %get-tuple-element.10.table_hbm, f32[3,3,256]{2,1,0:T(4,128)} %short.3, f32[1,256]{1,0:T(1,128)} %bitcast.13), custom_call_target="tpu_custom_call" | custom-call | tf_op jit(solution)/shard_map/edge/pallas_call | solution.py:401
  137.2 1.9 %collective-permute-start.3 = (bf16[160,256]{1,0:T(8,128)(2,1)}, bf16[160,256]{1,0:T(8,128)(2,1)S(1)}, u32[]{:S(2)}, u32[]{:S(2)}) collective-permute-start(bf16[160,256]{1,0:T(8,128)(2,1)} %edge.1.own_hbm), channel_id=1, source_target_pairs={{0,1},{1,0},{2,3},{3,2},{4,5},{5,4},{6,7},{7,6},{8,9},{9,8},{10,11... | collective-permute-start | bytes 245768 | tf_op jit(solution)/shard_map/ppermute | solution.py:25
  139.2 4.6 %collective-permute-done.3.oth = bf16[160,256]{1,0:T(8,128)(2,1)S(1)} collective-permute-done((bf16[160,256]{1,0:T(8,128)(2,1)}, bf16[160,256]{1,0:T(8,128)(2,1)S(1)}, u32[]{:S(2)}, u32[]{:S(2)}) %collective-permute-start.3) | collective-permute-done | bytes 81952 | tf_op jit(solution)/shard_map/ppermute | solution.py:25
  143.8 3.7 %shard_map.64 = bf16[8,160,256]{2,1,0:T(8,128)(2,1)} custom-call(s32[1]{0:T(128)} %bitcast.x_ref, bf16[160,256]{1,0:T(8,128)(2,1)} %edge.1.own_hbm, bf16[160,256]{1,0:T(8,128)(2,1)S(1)} %collective-permute-done.3.oth, bf16[256,4096]{1,0:T(8,128)(2,1)} %weight_hbm.5, bf16[8,256,256]{2,1,0:T(8,128)(2,1)} %copy-done), custom_call_target="tpu_custom_call" | custom-call | tf_op jit(solution)/shard_map/pallas_call | solution.py:381
  147.6 6.9 %all-to-all-start.2 = ((bf16[8,160,256]{2,1,0:T(8,128)(2,1)}), bf16[8,160,256]{2,1,0:T(8,128)(2,1)S(1)}, u32[]{:S(2)}, u32[]{:S(2)}) async-start(bf16[8,160,256]{2,1,0:T(8,128)(2,1)} %shard_map.64), calls=%async_computation.2 | async-start | bytes 1310720 | tf_op jit(solution)/shard_map/all_to_all | solution.py:29
  154.5 0.1 reduce_sum.25
  154.6 14.6 %all-to-all-done.2 = bf16[8,160,256]{2,1,0:T(8,128)(2,1)S(1)} async-done(((bf16[8,160,256]{2,1,0:T(8,128)(2,1)}), bf16[8,160,256]{2,1,0:T(8,128)(2,1)S(1)}, u32[]{:S(2)}, u32[]{:S(2)}) %all-to-all-start.2) | async-done | bytes 655392 | tf_op jit(solution)/shard_map/all_to_all | solution.py:29
  169.3 0.7 pad_maximum_fusion
  (11 shorter events, 0.2 us)
Async XLA Ops:
  0.0 45.4 %copy-start.2 = (bf16[16,128]{1,0:T(8,128)(2,1)S(1)}, bf16[16,128]{1,0:T(8,128)(2,1)}, u32[]{:S(2)}) copy-start(bf16[16,128]{1,0:T(8,128)(2,1)} %param.9) | copy-start | bytes 12292
  1.9 30.7 %all-to-all-start.1 = ((bf16[8,192,256]{2,1,0:T(8,128)(2,1)}), bf16[8,192,256]{2,1,0:T(8,128)(2,1)S(1)}, u32[]{:S(2)}, u32[]{:S(2)}) async-start(bf16[8,192,256]{2,1,0:T(8,128)(2,1)} %top.1), calls=%async_computation.1 | async-start | bytes 1572864 | tf_op jit(solution)/shard_map/all_to_all | solution.py:29
  10.3 6.2 %collective-permute-start = (bf16[128,256]{1,0:T(8,128)(2,1)S(1)}, bf16[128,256]{1,0:T(8,128)(2,1)S(1)}, u32[]{:S(2)}, u32[]{:S(2)}) collective-permute-start(bf16[128,256]{1,0:T(8,128)(2,1)S(1)} %get-tuple-element.12), channel_id=1, source_target_pairs={{0,1},{1,0},{2,3},{3,2},{4,5},{5,4},{6,7},{7,6},{8,9},{9,8},{10,11... | collective-permute-start | bytes 196616 | tf_op jit(solution)/shard_map/ppermute | solution.py:25
  32.6 1.3 copy-start.1
  33.9 53.4 %all-to-all-start = ((bf16[8,2,128,256]{3,2,1,0:T(8,128)(2,1)}), bf16[8,2,128,256]{3,2,1,0:T(8,128)(2,1)S(1)}, u32[]{:S(2)}, u32[]{:S(2)}) async-start(bf16[8,2,128,256]{3,2,1,0:T(8,128)(2,1)} %broadcast_in_dim.13), calls=%async_computation | async-start | bytes 2097152 | tf_op jit(solution)/shard_map/all_to_all | solution.py:29
  39.6 58.7 %collective-permute-start.4 = (bf16[8,256,256]{2,1,0:T(8,128)(2,1)}, bf16[8,256,256]{2,1,0:T(8,128)(2,1)S(1)}, u32[]{:S(2)}, u32[]{:S(2)}) collective-permute-start(bf16[8,256,256]{2,1,0:T(8,128)(2,1)} %slab.1), channel_id=1, source_target_pairs={{0,1},{1,0},{2,3},{3,2},{4,5},{5,4},{6,7},{7,6},{8,9},{9,8},{10,11... | collective-permute-start | bytes 3145736 | tf_op jit(solution)/shard_map/ppermute | solution.py:25
  42.9 40.7 %collective-permute-start.1 = (bf16[8,192,256]{2,1,0:T(8,128)(2,1)}, bf16[8,192,256]{2,1,0:T(8,128)(2,1)S(1)}, u32[]{:S(2)}, u32[]{:S(2)}) collective-permute-start(bf16[8,192,256]{2,1,0:T(8,128)(2,1)} %copy-done.1), channel_id=1, source_target_pairs={{0,1},{1,0},{2,3},{3,2},{4,5},{5,4},{6,7},{7,6},{8,9},{9,8},{10,11... | collective-permute-start | bytes 2359304 | tf_op jit(solution)/shard_map/ppermute | solution.py:25
  94.9 6.5 %collective-permute-start.5 = (bf16[160,256]{1,0:T(8,128)(2,1)}, bf16[160,256]{1,0:T(8,128)(2,1)S(1)}, u32[]{:S(2)}, u32[]{:S(2)}) collective-permute-start(bf16[160,256]{1,0:T(8,128)(2,1)} %inner.1.own_hbm), channel_id=1, source_target_pairs={{0,1},{1,0},{2,3},{3,2},{4,5},{5,4},{6,7},{7,6},{8,9},{9,8},{10,11... | collective-permute-start | bytes 245768 | tf_op jit(solution)/shard_map/ppermute | solution.py:25
  98.3 3.2 %copy-start = (bf16[8,256,256]{2,1,0:T(8,128)(2,1)}, bf16[8,256,256]{2,1,0:T(8,128)(2,1)S(1)}, u32[]{:S(2)}) copy-start(bf16[8,256,256]{2,1,0:T(8,128)(2,1)S(1)} %collective-permute-done.4.slab_hbm) | copy-start | bytes 3145732
  105.2 42.3 %all-to-all-start.3 = ((bf16[8,160,256]{2,1,0:T(8,128)(2,1)}), bf16[8,160,256]{2,1,0:T(8,128)(2,1)S(1)}, u32[]{:S(2)}, u32[]{:S(2)}) async-start(bf16[8,160,256]{2,1,0:T(8,128)(2,1)} %shard_map.65), calls=%async_computation.3 | async-start | bytes 1310720 | tf_op jit(solution)/shard_map/all_to_all | solution.py:29
  112.1 22.1 %collective-permute-start.2 = (bf16[136,768]{1,0:T(8,128)(2,1)}, bf16[136,768]{1,0:T(8,128)(2,1)S(1)}, u32[]{:S(2)}, u32[]{:S(2)}) collective-permute-start(bf16[136,768]{1,0:T(8,128)(2,1)} %late.1.tail_hbm), channel_id=1, source_target_pairs={{0,16},{16,32},{32,48},{48,64},{64,80},{80,96},{96,112},{112,128},... | collective-permute-start | bytes 626696 | tf_op jit(solution)/shard_map/ppermute | solution.py:34
  137.2 6.5 %collective-permute-start.3 = (bf16[160,256]{1,0:T(8,128)(2,1)}, bf16[160,256]{1,0:T(8,128)(2,1)S(1)}, u32[]{:S(2)}, u32[]{:S(2)}) collective-permute-start(bf16[160,256]{1,0:T(8,128)(2,1)} %edge.1.own_hbm), channel_id=1, source_target_pairs={{0,1},{1,0},{2,3},{3,2},{4,5},{5,4},{6,7},{7,6},{8,9},{9,8},{10,11... | collective-permute-start | bytes 245768 | tf_op jit(solution)/shard_map/ppermute | solution.py:25
  147.6 21.6 %all-to-all-start.2 = ((bf16[8,160,256]{2,1,0:T(8,128)(2,1)}), bf16[8,160,256]{2,1,0:T(8,128)(2,1)S(1)}, u32[]{:S(2)}, u32[]{:S(2)}) async-start(bf16[8,160,256]{2,1,0:T(8,128)(2,1)} %shard_map.64), calls=%async_computation.2 | async-start | bytes 1310720 | tf_op jit(solution)/shard_map/all_to_all | solution.py:29
